TPU v7x, 32 devices: a whole 2x2x4 slice. The times are simulated.
32 devices in a mesh: groups: 2 (over x), ctx: 16 (over z, y, core).
Axes of the slice: x: 2, y: 2, z: 4, core: 2. Of those that a mesh axis runs over, the one named last changes fastest.
Arguments:
- query_video: bfloat16 [12288, 1536], P(('groups', 'ctx')), parts along dimension 0, may hold values from -10 to 10
- key_video: bfloat16 [12288, 1536], P(('groups', 'ctx')), parts along dimension 0, may hold values from -5 to 5
- value_video: bfloat16 [12288, 1536], P(('groups', 'ctx')), parts along dimension 0, may hold values from -6 to 6
- query_text: bfloat16 [512, 1536], P(('groups', 'ctx')), parts along dimension 0, may hold values from -10 to 10
- key_text: bfloat16 [512, 1536], P(('groups', 'ctx')), parts along dimension 0, may hold values from -5 to 5
- value_text: bfloat16 [512, 1536], P(('groups', 'ctx')), parts along dimension 0, may hold values from -6 to 6
- key_tiles: int32 [32, 3], P(('groups', 'ctx')), parts along dimension 0, may hold values from 0 to 15, as said below
- tile_owner: int32 [32], P('groups'), parts along dimension 0, may hold values from 0 to 15, as said below
- text_count: int32 [2], P('groups'), parts along dimension 0, may hold values from 64 to 256
Outputs:
- video_out: bfloat16 [12288, 1536], P(('groups', 'ctx')), parts along dimension 0
- text_out: bfloat16 [512, 1536], P(('groups', 'ctx')), parts along dimension 0
There are 2 independent parts, one for each index of `groups`. A program takes and returns all parts, laid end to end along the dimension named above; each array names one. Nothing has to cross between parts.
Inputs may be any that keep to these rules, and one draw needn't show every extreme that they name: `key_tiles`: each list names 3 different tiles, the query tile itself among them; every listed tile has a stored position whose device (position) is at most 2 away from the query tile's device, and every list names one exactly 2 away. `tile_owner`: A permutation of the tile numbers.
All inputs are finite; a program needn't handle non-finite values.
Results may differ from a plain program's by a relative error of at most 0.0032.
Values may be sent and summed in bfloat16 or wider, within the bound.
A program may use at most 384 MiB of HBM per device.

v0:
```python
import math

import jax
import jax.numpy as jnp
from jax import lax
from jax.sharding import PartitionSpec as P

TILE = 384
HD = 128
NB = 3
REACH = 2


def shifted(shard, axis, by):
    count = lax.axis_size(axis)
    pairs = [(i, i + by) for i in range(count) if 0 <= i + by < count]
    return lax.ppermute(shard, axis, pairs)


def combined_all(value, axis, join):
    pieces = jax.tree.map(lambda part: lax.all_gather(part, axis), value)
    head = jax.tree.map(lambda part: part[0], pieces)
    tail = jax.tree.map(lambda part: part[1:], pieces)
    total, _ = lax.scan(lambda total, share: (join(total, share), None), head, tail)
    return total


def spread_heads(values):
    return jnp.repeat(values, HD, axis=1)


def combine_parts(earlier_part, later_part):
    max_early, total_early, acc_early = earlier_part
    max_late, total_late, acc_late = later_part
    joint_max = jnp.maximum(max_early, max_late)
    factor_early = jnp.exp(max_early - joint_max)
    factor_late = jnp.exp(max_late - joint_max)
    joint_total = total_early * factor_early + total_late * factor_late
    joint_acc = acc_early * spread_heads(factor_early) + acc_late * spread_heads(factor_late)
    return (joint_max, joint_total, joint_acc)


def on_device(
    query_video,
    key_video,
    value_video,
    query_text,
    key_text,
    value_text,
    key_tiles,
    tile_owner,
    text_count,
):
    ctx_rank = lax.axis_index("ctx")
    row_count, feature_width = query_video.shape
    head_count = feature_width // HD
    tiles_here = row_count // TILE
    text_here = query_text.shape[0]
    inverse_root_dimension = 1.0 / math.sqrt(HD)
    text_query, text_keys, text_values = (
        lax.all_gather(query_text, "ctx", axis=0, tiled=True),
        lax.all_gather(key_text, "ctx", axis=0, tiled=True),
        lax.all_gather(value_text, "ctx", axis=0, tiled=True),
    )
    text_rows = text_keys.shape[0]
    text_limit = text_count[0]
    text_ok = jnp.arange(text_rows) < text_limit
    local_ok = ctx_rank * text_here + jnp.arange(text_here) < text_limit
    own_pair = (key_video, value_video)
    fetched = {}
    for offset in [value for value in range(-REACH, REACH + 1) if value != 0]:
        fetched[offset] = shifted((own_pair[0], own_pair[1]), "ctx", -offset)
    fetched[0] = own_pair
    window_keys = jnp.concatenate(
        [fetched[offset][0] for offset in range(-REACH, REACH + 1)], axis=0
    )
    window_values = jnp.concatenate(
        [fetched[offset][1] for offset in range(-REACH, REACH + 1)], axis=0
    )
    window_tiles = (2 * REACH + 1) * tiles_here
    tile_count = tile_owner.shape[0]
    matches = key_tiles[:, :, None] == jnp.arange(tile_count, dtype=jnp.int32)[None, None, :]
    key_slots = jnp.sum(jnp.where(matches, tile_owner[None, None, :], 0), axis=-1)
    window_index = key_slots - (ctx_rank - REACH) * tiles_here

    def head_step(head_index, carry_state):
        video_buffer, text_max, text_sum, text_acc = carry_state
        column_start = head_index * HD
        query_head = lax.dynamic_slice_in_dim(query_video, column_start, HD, 1).reshape(
            tiles_here, TILE, HD
        )
        key_window = lax.dynamic_slice_in_dim(window_keys, column_start, HD, 1).reshape(
            window_tiles, TILE, HD
        )
        value_window = lax.dynamic_slice_in_dim(window_values, column_start, HD, 1).reshape(
            window_tiles, TILE, HD
        )
        key_near = key_window[window_index].reshape(tiles_here, NB * TILE, HD)
        value_near = value_window[window_index].reshape(tiles_here, NB * TILE, HD)
        key_words = lax.dynamic_slice_in_dim(text_keys, column_start, HD, 1)
        value_words = lax.dynamic_slice_in_dim(text_values, column_start, HD, 1)
        frame_affinity_array = (
            jnp.einsum("tqd,tkd->tqk", query_head, key_near, preferred_element_type=jnp.float32)
            * inverse_root_dimension
        )
        wording_affinity_array = (
            jnp.einsum("tqd,kd->tqk", query_head, key_words, preferred_element_type=jnp.float32)
            * inverse_root_dimension
        )
        wording_affinity_array = jnp.where(text_ok[None, None, :], wording_affinity_array, -jnp.inf)
        row_max = jnp.maximum(
            jnp.max(frame_affinity_array, axis=-1, keepdims=True),
            jnp.max(wording_affinity_array, axis=-1, keepdims=True),
        )
        weight_video = jnp.exp(frame_affinity_array - row_max)
        weight_text = jnp.exp(wording_affinity_array - row_max)
        row_total = jnp.sum(weight_video, axis=-1) + jnp.sum(weight_text, axis=-1)
        mixed_values = jnp.einsum(
            "tqk,tkd->tqd",
            weight_video.astype(jnp.bfloat16),
            value_near,
            preferred_element_type=jnp.float32,
        )
        mixed_values = mixed_values + jnp.einsum(
            "tqk,kd->tqd",
            weight_text.astype(jnp.bfloat16),
            value_words,
            preferred_element_type=jnp.float32,
        )
        head_output = (
            (mixed_values / row_total[:, :, None]).astype(jnp.bfloat16).reshape(row_count, HD)
        )
        video_buffer = lax.dynamic_update_slice_in_dim(video_buffer, head_output, column_start, 1)
        text_head = lax.dynamic_slice_in_dim(text_query, column_start, HD, 1)
        key_local = lax.dynamic_slice_in_dim(key_video, column_start, HD, 1)
        value_local = lax.dynamic_slice_in_dim(value_video, column_start, HD, 1)
        key_own_text = lax.dynamic_slice_in_dim(key_text, column_start, HD, 1)
        value_own_text = lax.dynamic_slice_in_dim(value_text, column_start, HD, 1)
        score_local = (
            jnp.einsum("td,kd->tk", text_head, key_local, preferred_element_type=jnp.float32)
            * inverse_root_dimension
        )
        score_own = (
            jnp.einsum("td,kd->tk", text_head, key_own_text, preferred_element_type=jnp.float32)
            * inverse_root_dimension
        )
        score_own = jnp.where(local_ok[None, :], score_own, -jnp.inf)
        block_max = jnp.maximum(jnp.max(score_local, axis=-1), jnp.max(score_own, axis=-1))
        weight_local = jnp.exp(score_local - block_max[:, None])
        weight_own = jnp.exp(score_own - block_max[:, None])
        block_total = jnp.sum(weight_local, axis=-1) + jnp.sum(weight_own, axis=-1)
        block_acc = jnp.einsum(
            "tk,kd->td",
            weight_local.astype(jnp.bfloat16),
            value_local,
            preferred_element_type=jnp.float32,
        )
        block_acc = block_acc + jnp.einsum(
            "tk,kd->td",
            weight_own.astype(jnp.bfloat16),
            value_own_text,
            preferred_element_type=jnp.float32,
        )
        text_max = lax.dynamic_update_slice(text_max, block_max[:, None], (0, head_index))
        text_sum = lax.dynamic_update_slice(text_sum, block_total[:, None], (0, head_index))
        text_acc = lax.dynamic_update_slice_in_dim(text_acc, block_acc, column_start, 1)
        return (video_buffer, text_max, text_sum, text_acc)

    initial_state = (
        jnp.zeros((row_count, feature_width), jnp.bfloat16),
        jnp.zeros((text_rows, head_count), jnp.float32),
        jnp.zeros((text_rows, head_count), jnp.float32),
        jnp.zeros((text_rows, feature_width), jnp.float32),
    )
    video_out, text_max, text_sum, text_acc = lax.fori_loop(0, head_count, head_step, initial_state)
    joint_max, joint_total, joint_acc = combined_all(
        (text_max, text_sum, text_acc), "ctx", combine_parts
    )
    own_total = lax.dynamic_slice_in_dim(joint_total, ctx_rank * text_here, text_here, 0)
    own_acc = lax.dynamic_slice_in_dim(joint_acc, ctx_rank * text_here, text_here, 0)
    text_out = (own_acc / spread_heads(own_total)).astype(jnp.bfloat16)
    return (video_out, text_out)


def solution(mesh):
    return jax.shard_map(
        on_device,
        mesh=mesh,
        in_specs=(
            P(("groups", "ctx"), None),
            P(("groups", "ctx"), None),
            P(("groups", "ctx"), None),
            P(("groups", "ctx"), None),
            P(("groups", "ctx"), None),
            P(("groups", "ctx"), None),
            P(("groups", "ctx"), None),
            P("groups"),
            P("groups"),
        ),
        out_specs=(P(("groups", "ctx"), None), P(("groups", "ctx"), None)),
        check_vma=False,
    )
```

profile of v0, /device:TPU:15, one launch (start us, length us, event | category | flops | bytes accessed | tf_op | source)
XLA Modules:
  0.0 656.8 jit_solution(15291442228963987204)
XLA Ops:
  7.3 3.3 collective-permute-start
  10.5 4.0 collective-permute-start.1
  14.5 1.9 collective-permute-start.2
  16.5 3.2 collective-permute-start.4
  19.6 3.9 collective-permute-start.5
  23.6 93.0 %all_gather.27 = bf16[256,1536]{1,0:T(8,128)(2,1)S(1)} all-gather(bf16[16,1536]{1,0:T(8,128)(2,1)} %param.17), channel_id=1, replica_groups=mesh['groups'=2,'ctx'=16] {'ctx'}, dimensions={0}, use_global_device_ids=true | all-gather | bytes 835584 | tf_op jit(solution)/shard_map/all_gather | solution.py:62
  116.5 19.2 %all_gather.28 = bf16[256,1536]{1,0:T(8,128)(2,1)} all-gather(bf16[16,1536]{1,0:T(8,128)(2,1)} %param.18), channel_id=1, replica_groups=mesh['groups'=2,'ctx'=16] {'ctx'}, dimensions={0}, use_global_device_ids=true | all-gather | bytes 835584 | tf_op jit(solution)/shard_map/all_gather | solution.py:63
  135.8 24.3 %all_gather.29 = bf16[256,1536]{1,0:T(8,128)(2,1)} all-gather(bf16[16,1536]{1,0:T(8,128)(2,1)S(1)} %copy-done.12), channel_id=1, replica_groups=mesh['groups'=2,'ctx'=16] {'ctx'}, dimensions={0}, use_global_device_ids=true | all-gather | bytes 835584 | tf_op jit(solution)/shard_map/all_gather | solution.py:61
  160.3 1.9 collective-permute-start.3
  163.6 2.3 collective-permute-start.6
  167.4 6.2 collective-permute-start.7
  177.7 12.8 %collective-permute-done.3 = bf16[384,1536]{1,0:T(8,128)(2,1)S(1)} collective-permute-done((bf16[384,1536]{1,0:T(8,128)(2,1)S(1)}, bf16[384,1536]{1,0:T(8,128)(2,1)S(1)}, u32[]{:S(2)}, u32[]{:S(2)}) %collective-permute-start.3) | collective-permute-done | bytes 1179680 | tf_op jit(solution)/shard_map/ppermute | solution.py:17
  190.6 25.5 %collective-permute-done.6 = bf16[384,1536]{1,0:T(8,128)(2,1)S(1)} collective-permute-done((bf16[384,1536]{1,0:T(8,128)(2,1)}, bf16[384,1536]{1,0:T(8,128)(2,1)S(1)}, u32[]{:S(2)}, u32[]{:S(2)}) %collective-permute-start.6) | collective-permute-done | bytes 1179680 | tf_op jit(solution)/shard_map/ppermute | solution.py:17
  216.3 1.5 broadcast_in_dim.102
  217.8 1.6 broadcast_in_dim.101
  219.6 179.9 %while.36 = (s32[]{:T(128)}, bf16[384,1536]{1,0:T(8,128)(2,1)}, f32[256,12]{0,1:T(8,128)S(1)}, f32[256,12]{0,1:T(8,128)S(1)}, f32[256,1536]{1,0:T(8,128)}, /*ind...) while((s32[]{:T(128)}, bf16[384,1536]{1,0:T(8,128)(2,1)}, ...), condition=%wide.region_10.11_spmd.clone.clone, body=%wide.region_1.10_spmd.clone.clone.sunk | while | flops 333393952 | bytes 24062668 | solution.py:175
  226.6 1.9 fusion.103
  232.3 1.9 fusion.109
  234.6 1.5 constant_dynamic-slice_fusion.11
  241.6 1.9 fusion.103
  247.3 1.9 fusion.109
  249.6 1.5 constant_dynamic-slice_fusion.11
  256.6 1.9 fusion.103
  262.3 1.9 fusion.109
  271.6 1.9 fusion.103
  277.3 1.9 fusion.109
  286.6 1.9 fusion.103
  292.3 1.8 fusion.109
  301.6 1.9 fusion.103
  307.3 1.8 fusion.109
  316.6 1.9 fusion.103
  322.3 1.8 fusion.109
  331.5 1.9 fusion.103
  337.3 1.9 fusion.109
  346.5 1.9 fusion.103
  352.3 1.9 fusion.109
  361.5 1.9 fusion.103
  367.3 1.9 fusion.109
  376.5 1.9 fusion.103
  382.3 1.9 fusion.109
  391.6 1.9 fusion.103
  397.3 1.9 fusion.109
  399.6 31.0 %all-gather = f32[4096,12]{0,1:T(8,128)S(1)} all-gather(f32[256,12]{0,1:T(8,128)S(1)} %get-tuple-element.794), channel_id=2, replica_groups=mesh['groups'=2,'ctx'=16] {'ctx'}, dimensions={0}, use_global_device_ids=true | all-gather | bytes 208896 | tf_op jit(solution)/shard_map/all_gather | solution.py:21
  430.6 21.5 %all-gather.1 = f32[4096,12]{0,1:T(8,128)S(1)} all-gather(f32[256,12]{0,1:T(8,128)S(1)} %get-tuple-element.795), channel_id=3, replica_groups=mesh['groups'=2,'ctx'=16] {'ctx'}, dimensions={0}, use_global_device_ids=true | all-gather | bytes 208896 | tf_op jit(solution)/shard_map/all_gather | solution.py:21
  452.3 92.0 %all-gather.5.cloned.1.call-done = f32[4096,1536]{1,0:T(8,128)} async-done(((f32[256,1536]{1,0:T(8,128)}), f32[4096,1536]{1,0:T(8,128)}) %all-gather.5.cloned.1.call-update) | async-done | bytes 25165840 | tf_op jit(solution)/shard_map/all_gather | solution.py:21
  545.7 1.6 copy.22
  547.3 16.3 %slice.39 = f32[3840,1536]{1,0:T(8,128)} slice(f32[4096,1536]{1,0:T(8,128)} %all-gather.5.cloned.1.call-done), slice={[256:4096], [0:1536]} | slice | bytes 47185920 | tf_op jit(solution)/shard_map/slice | solution.py:23
  563.6 83.5 %while.35 = (s32[]{:T(128)}, f32[256,12]{0,1:T(8,128)S(1)}, f32[256,12]{0,1:T(8,128)S(1)}, f32[256,1536]{0,1:T(8,128)}, f32[15,256,12]{1,0,2:T(8,128)S(1)}, /*in...) while((s32[]{:T(128)}, f32[256,12]{0,1:T(8,128)S(1)}, f32[256,12]{0,1:T(8,128)S(1)}, ...), condition=%wide.region_12.13_spmd, body=%wide.region_11.12_spmd.sunk | while | flops 1198082 | bytes 14131405 | solution.py:24
  566.3 2.8 fusion.87
  571.9 2.8 fusion.87
  577.5 2.8 fusion.87
  583.0 2.8 fusion.87
  588.6 2.8 fusion.87
  594.2 2.8 fusion.87
  599.7 2.8 fusion.87
  605.3 2.8 fusion.87
  610.9 2.8 fusion.87
  616.4 2.8 fusion.87
  622.0 2.8 fusion.87
  627.6 2.8 fusion.87
  633.2 2.8 fusion.87
  638.7 2.8 fusion.87
  644.3 2.8 fusion.87
  647.3 1.9 copy.26
  (578 shorter events, 180.5 us)
Async XLA Ops:
  7.2 153.1 %copy-start = (bf16[384,1536]{1,0:T(8,128)(2,1)S(1)}, bf16[384,1536]{1,0:T(8,128)(2,1)}, u32[]{:S(2)}) copy-start(bf16[384,1536]{1,0:T(8,128)(2,1)} %param.14) | copy-start | bytes 3538948
  7.2 128.6 %copy-start.12 = (bf16[16,1536]{1,0:T(8,128)(2,1)S(1)}, bf16[16,1536]{1,0:T(8,128)(2,1)}, u32[]{:S(2)}) copy-start(bf16[16,1536]{1,0:T(8,128)(2,1)} %param.16) | copy-start | bytes 147460
  7.2 152.9 %copy-start.13 = (s32[1,3]{1,0:T(1,128)S(1)}, s32[1,3]{1,0:T(1,128)}, u32[]{:S(2)}) copy-start(s32[1,3]{1,0:T(1,128)} %param.19) | copy-start | bytes 40
  7.2 152.8 %copy-start.14 = (s32[16]{0:T(128)S(1)}, s32[16]{0:T(128)}, u32[]{:S(2)}) copy-start(s32[16]{0:T(128)} %param.20) | copy-start | bytes 196
  7.2 537.1 %all-gather.5.cloned.1.call-start = ((), (), s32[]{:S(2)}) async-start(), calls=%async_computation | async-start | bytes 26738688 | tf_op jit(solution)/shard_map/all_gather | solution.py:21
  7.3 153.0 %collective-permute-start = (bf16[384,1536]{1,0:T(8,128)(2,1)}, bf16[384,1536]{1,0:T(8,128)(2,1)}, u32[]{:S(2)}, u32[]{:S(2)}) collective-permute-start(bf16[384,1536]{1,0:T(8,128)(2,1)} %param.14), channel_id=1, source_target_pairs={{0,2},{1,3},{2,4},{3,5},{4,6},{5,7},{6,8},{7,9},{8,10},{9,11},{10,... | collective-permute-start | bytes 3538952 | tf_op jit(solution)/shard_map/ppermute | solution.py:17
  10.5 153.0 %collective-permute-start.1 = (bf16[384,1536]{1,0:T(8,128)(2,1)}, bf16[384,1536]{1,0:T(8,128)(2,1)}, u32[]{:S(2)}, u32[]{:S(2)}) collective-permute-start(bf16[384,1536]{1,0:T(8,128)(2,1)} %param.14), channel_id=1, source_target_pairs={{0,1},{1,2},{2,3},{3,4},{4,5},{5,6},{6,7},{7,8},{8,9},{9,10},{10,1... | collective-permute-start | bytes 3538952 | tf_op jit(solution)/shard_map/ppermute | solution.py:17
  14.5 163.1 %collective-permute-start.2 = (bf16[384,1536]{1,0:T(8,128)(2,1)}, bf16[384,1536]{1,0:T(8,128)(2,1)S(1)}, u32[]{:S(2)}, u32[]{:S(2)}) collective-permute-start(bf16[384,1536]{1,0:T(8,128)(2,1)} %param.14), channel_id=1, source_target_pairs={{1,0},{2,1},{3,2},{4,3},{5,4},{6,5},{7,6},{8,7},{9,8},{10,9},{11,1... | collective-permute-start | bytes 3538952 | tf_op jit(solution)/shard_map/ppermute | solution.py:17
  16.5 150.9 %collective-permute-start.4 = (bf16[384,1536]{1,0:T(8,128)(2,1)}, bf16[384,1536]{1,0:T(8,128)(2,1)}, u32[]{:S(2)}, u32[]{:S(2)}) collective-permute-start(bf16[384,1536]{1,0:T(8,128)(2,1)} %param.15), channel_id=1, source_target_pairs={{0,2},{1,3},{2,4},{3,5},{4,6},{5,7},{6,8},{7,9},{8,10},{9,11},{10,... | collective-permute-start | bytes 3538952 | tf_op jit(solution)/shard_map/ppermute | solution.py:17
  19.6 155.3 %collective-permute-start.5 = (bf16[384,1536]{1,0:T(8,128)(2,1)}, bf16[384,1536]{1,0:T(8,128)(2,1)}, u32[]{:S(2)}, u32[]{:S(2)}) collective-permute-start(bf16[384,1536]{1,0:T(8,128)(2,1)} %param.15), channel_id=1, source_target_pairs={{0,1},{1,2},{2,3},{3,4},{4,5},{5,6},{6,7},{7,8},{8,9},{9,10},{10,1... | collective-permute-start | bytes 3538952 | tf_op jit(solution)/shard_map/ppermute | solution.py:17
  160.3 30.2 %collective-permute-start.3 = (bf16[384,1536]{1,0:T(8,128)(2,1)S(1)}, bf16[384,1536]{1,0:T(8,128)(2,1)S(1)}, u32[]{:S(2)}, u32[]{:S(2)}) collective-permute-start(bf16[384,1536]{1,0:T(8,128)(2,1)S(1)} %copy-done), channel_id=1, source_target_pairs={{2,0},{3,1},{4,2},{5,3},{6,4},{7,5},{8,6},{9,7},{10,8},{11,9},{12,... | collective-permute-start | bytes 3538952 | tf_op jit(solution)/shard_map/ppermute | solution.py:17
  163.6 52.5 %collective-permute-start.6 = (bf16[384,1536]{1,0:T(8,128)(2,1)}, bf16[384,1536]{1,0:T(8,128)(2,1)S(1)}, u32[]{:S(2)}, u32[]{:S(2)}) collective-permute-start(bf16[384,1536]{1,0:T(8,128)(2,1)} %param.15), channel_id=1, source_target_pairs={{1,0},{2,1},{3,2},{4,3},{5,4},{6,5},{7,6},{8,7},{9,8},{10,9},{11,1... | collective-permute-start | bytes 3538952 | tf_op jit(solution)/shard_map/ppermute | solution.py:17
  167.4 48.8 %collective-permute-start.7 = (bf16[384,1536]{1,0:T(8,128)(2,1)}, bf16[384,1536]{1,0:T(8,128)(2,1)S(1)}, u32[]{:S(2)}, u32[]{:S(2)}) collective-permute-start(bf16[384,1536]{1,0:T(8,128)(2,1)} %param.15), channel_id=1, source_target_pairs={{2,0},{3,1},{4,2},{5,3},{6,4},{7,5},{8,6},{9,7},{10,8},{11,9},{12,... | collective-permute-start | bytes 3538952 | tf_op jit(solution)/shard_map/ppermute | solution.py:17
  190.6 28.8 %copy-start.2 = (bf16[1920,1536]{1,0:T(8,128)(2,1)}, bf16[1920,1536]{1,0:T(8,128)(2,1)S(1)}, u32[]{:S(2)}) copy-start(bf16[1920,1536]{1,0:T(8,128)(2,1)S(1)} %constant_dynamic-update-slice_fusion) | copy-start | bytes 17694724
  216.2 3.4 copy-start.3
  219.6 4.3 copy-start.4
  226.6 7.9 %copy-start.1 = (bf16[384,1536]{1,0:T(8,128)(2,1)S(1)}, bf16[384,1536]{1,0:T(8,128)(2,1)}, u32[]{:S(2)}) copy-start(bf16[384,1536]{1,0:T(8,128)(2,1)} %get-tuple-element.814) | copy-start | bytes 3538948 | tf_op jit(solution)/shard_map/while
  226.6 7.9 %copy-start.5 = (bf16[256,1536]{1,0:T(8,128)(2,1)S(1)}, bf16[256,1536]{1,0:T(8,128)(2,1)}, u32[]{:S(2)}) copy-start(bf16[256,1536]{1,0:T(8,128)(2,1)} %copy-done.4) | copy-start | bytes 2359300 | tf_op jit(solution)/shard_map/while
  234.6 4.3 copy-start.4
  241.6 8.0 %copy-start.1 = (bf16[384,1536]{1,0:T(8,128)(2,1)S(1)}, bf16[384,1536]{1,0:T(8,128)(2,1)}, u32[]{:S(2)}) copy-start(bf16[384,1536]{1,0:T(8,128)(2,1)} %get-tuple-element.814) | copy-start | bytes 3538948 | tf_op jit(solution)/shard_map/while
  241.6 8.0 %copy-start.5 = (bf16[256,1536]{1,0:T(8,128)(2,1)S(1)}, bf16[256,1536]{1,0:T(8,128)(2,1)}, u32[]{:S(2)}) copy-start(bf16[256,1536]{1,0:T(8,128)(2,1)} %copy-done.4) | copy-start | bytes 2359300 | tf_op jit(solution)/shard_map/while
  249.6 4.3 copy-start.4
  256.6 8.0 %copy-start.1 = (bf16[384,1536]{1,0:T(8,128)(2,1)S(1)}, bf16[384,1536]{1,0:T(8,128)(2,1)}, u32[]{:S(2)}) copy-start(bf16[384,1536]{1,0:T(8,128)(2,1)} %get-tuple-element.814) | copy-start | bytes 3538948 | tf_op jit(solution)/shard_map/while
  256.6 8.0 %copy-start.5 = (bf16[256,1536]{1,0:T(8,128)(2,1)S(1)}, bf16[256,1536]{1,0:T(8,128)(2,1)}, u32[]{:S(2)}) copy-start(bf16[256,1536]{1,0:T(8,128)(2,1)} %copy-done.4) | copy-start | bytes 2359300 | tf_op jit(solution)/shard_map/while
  264.6 4.3 copy-start.4
  271.6 7.9 %copy-start.1 = (bf16[384,1536]{1,0:T(8,128)(2,1)S(1)}, bf16[384,1536]{1,0:T(8,128)(2,1)}, u32[]{:S(2)}) copy-start(bf16[384,1536]{1,0:T(8,128)(2,1)} %get-tuple-element.814) | copy-start | bytes 3538948 | tf_op jit(solution)/shard_map/while
  271.6 7.9 %copy-start.5 = (bf16[256,1536]{1,0:T(8,128)(2,1)S(1)}, bf16[256,1536]{1,0:T(8,128)(2,1)}, u32[]{:S(2)}) copy-start(bf16[256,1536]{1,0:T(8,128)(2,1)} %copy-done.4) | copy-start | bytes 2359300 | tf_op jit(solution)/shard_map/while
  279.6 4.3 copy-start.4
  286.6 7.9 %copy-start.1 = (bf16[384,1536]{1,0:T(8,128)(2,1)S(1)}, bf16[384,1536]{1,0:T(8,128)(2,1)}, u32[]{:S(2)}) copy-start(bf16[384,1536]{1,0:T(8,128)(2,1)} %get-tuple-element.814) | copy-start | bytes 3538948 | tf_op jit(solution)/shard_map/while
  286.6 7.9 %copy-start.5 = (bf16[256,1536]{1,0:T(8,128)(2,1)S(1)}, bf16[256,1536]{1,0:T(8,128)(2,1)}, u32[]{:S(2)}) copy-start(bf16[256,1536]{1,0:T(8,128)(2,1)} %copy-done.4) | copy-start | bytes 2359300 | tf_op jit(solution)/shard_map/while
  294.5 4.3 copy-start.4
  301.6 7.9 %copy-start.1 = (bf16[384,1536]{1,0:T(8,128)(2,1)S(1)}, bf16[384,1536]{1,0:T(8,128)(2,1)}, u32[]{:S(2)}) copy-start(bf16[384,1536]{1,0:T(8,128)(2,1)} %get-tuple-element.814) | copy-start | bytes 3538948 | tf_op jit(solution)/shard_map/while
  301.6 7.9 %copy-start.5 = (bf16[256,1536]{1,0:T(8,128)(2,1)S(1)}, bf16[256,1536]{1,0:T(8,128)(2,1)}, u32[]{:S(2)}) copy-start(bf16[256,1536]{1,0:T(8,128)(2,1)} %copy-done.4) | copy-start | bytes 2359300 | tf_op jit(solution)/shard_map/while
  309.5 4.3 copy-start.4
  316.5 7.9 %copy-start.1 = (bf16[384,1536]{1,0:T(8,128)(2,1)S(1)}, bf16[384,1536]{1,0:T(8,128)(2,1)}, u32[]{:S(2)}) copy-start(bf16[384,1536]{1,0:T(8,128)(2,1)} %get-tuple-element.814) | copy-start | bytes 3538948 | tf_op jit(solution)/shard_map/while
  316.6 7.9 %copy-start.5 = (bf16[256,1536]{1,0:T(8,128)(2,1)S(1)}, bf16[256,1536]{1,0:T(8,128)(2,1)}, u32[]{:S(2)}) copy-start(bf16[256,1536]{1,0:T(8,128)(2,1)} %copy-done.4) | copy-start | bytes 2359300 | tf_op jit(solution)/shard_map/while
  324.5 4.3 copy-start.4
  331.5 8.0 %copy-start.1 = (bf16[384,1536]{1,0:T(8,128)(2,1)S(1)}, bf16[384,1536]{1,0:T(8,128)(2,1)}, u32[]{:S(2)}) copy-start(bf16[384,1536]{1,0:T(8,128)(2,1)} %get-tuple-element.814) | copy-start | bytes 3538948 | tf_op jit(solution)/shard_map/while
  331.5 8.0 %copy-start.5 = (bf16[256,1536]{1,0:T(8,128)(2,1)S(1)}, bf16[256,1536]{1,0:T(8,128)(2,1)}, u32[]{:S(2)}) copy-start(bf16[256,1536]{1,0:T(8,128)(2,1)} %copy-done.4) | copy-start | bytes 2359300 | tf_op jit(solution)/shard_map/while
  339.5 4.3 copy-start.4
  346.5 8.0 %copy-start.1 = (bf16[384,1536]{1,0:T(8,128)(2,1)S(1)}, bf16[384,1536]{1,0:T(8,128)(2,1)}, u32[]{:S(2)}) copy-start(bf16[384,1536]{1,0:T(8,128)(2,1)} %get-tuple-element.814) | copy-start | bytes 3538948 | tf_op jit(solution)/shard_map/while
  346.5 8.0 %copy-start.5 = (bf16[256,1536]{1,0:T(8,128)(2,1)S(1)}, bf16[256,1536]{1,0:T(8,128)(2,1)}, u32[]{:S(2)}) copy-start(bf16[256,1536]{1,0:T(8,128)(2,1)} %copy-done.4) | copy-start | bytes 2359300 | tf_op jit(solution)/shard_map/while
  354.5 4.3 copy-start.4
  361.5 8.0 %copy-start.1 = (bf16[384,1536]{1,0:T(8,128)(2,1)S(1)}, bf16[384,1536]{1,0:T(8,128)(2,1)}, u32[]{:S(2)}) copy-start(bf16[384,1536]{1,0:T(8,128)(2,1)} %get-tuple-element.814) | copy-start | bytes 3538948 | tf_op jit(solution)/shard_map/while
  361.5 8.0 %copy-start.5 = (bf16[256,1536]{1,0:T(8,128)(2,1)S(1)}, bf16[256,1536]{1,0:T(8,128)(2,1)}, u32[]{:S(2)}) copy-start(bf16[256,1536]{1,0:T(8,128)(2,1)} %copy-done.4) | copy-start | bytes 2359300 | tf_op jit(solution)/shard_map/while
  369.5 4.3 copy-start.4
  376.5 8.0 %copy-start.1 = (bf16[384,1536]{1,0:T(8,128)(2,1)S(1)}, bf16[384,1536]{1,0:T(8,128)(2,1)}, u32[]{:S(2)}) copy-start(bf16[384,1536]{1,0:T(8,128)(2,1)} %get-tuple-element.814) | copy-start | bytes 3538948 | tf_op jit(solution)/shard_map/while
  376.5 8.0 %copy-start.5 = (bf16[256,1536]{1,0:T(8,128)(2,1)S(1)}, bf16[256,1536]{1,0:T(8,128)(2,1)}, u32[]{:S(2)}) copy-start(bf16[256,1536]{1,0:T(8,128)(2,1)} %copy-done.4) | copy-start | bytes 2359300 | tf_op jit(solution)/shard_map/while
  384.5 4.3 copy-start.4
  391.5 8.0 %copy-start.1 = (bf16[384,1536]{1,0:T(8,128)(2,1)S(1)}, bf16[384,1536]{1,0:T(8,128)(2,1)}, u32[]{:S(2)}) copy-start(bf16[384,1536]{1,0:T(8,128)(2,1)} %get-tuple-element.814) | copy-start | bytes 3538948 | tf_op jit(solution)/shard_map/while
  391.6 8.0 %copy-start.5 = (bf16[256,1536]{1,0:T(8,128)(2,1)S(1)}, bf16[256,1536]{1,0:T(8,128)(2,1)}, u32[]{:S(2)}) copy-start(bf16[256,1536]{1,0:T(8,128)(2,1)} %copy-done.4) | copy-start | bytes 2359300 | tf_op jit(solution)/shard_map/while
  430.6 113.7 %copy-start.6 = (f32[4096,12]{0,1:T(8,128)}, f32[4096,12]{0,1:T(8,128)S(1)}, u32[]{:S(2)}) copy-start(f32[4096,12]{0,1:T(8,128)S(1)} %all-gather) | copy-start | bytes 589828
  452.1 92.1 %copy-start.7 = (f32[4096,12]{0,1:T(8,128)}, f32[4096,12]{0,1:T(8,128)S(1)}, u32[]{:S(2)}) copy-start(f32[4096,12]{0,1:T(8,128)S(1)} %all-gather.1) | copy-start | bytes 589828
  547.3 16.3 %slice-start.1 = ((f32[4096,12]{0,1:T(8,128)}), f32[256,12]{0,1:T(8,128)S(1)}, s32[]{:S(2)}) async-start(f32[4096,12]{0,1:T(8,128)} %copy-done.6), calls=%async_computation.2 | async-start | bytes 32768 | tf_op jit(solution)/shard_map/slice | solution.py:22
  547.3 16.3 %slice-start.2 = ((f32[4096,12]{0,1:T(8,128)}), f32[256,12]{0,1:T(8,128)S(1)}, s32[]{:S(2)}) async-start(f32[4096,12]{0,1:T(8,128)} %copy-done.7), calls=%async_computation.3 | async-start | bytes 32768 | tf_op jit(solution)/shard_map/slice | solution.py:22
  566.3 2.8 copy-start.9
  571.9 2.8 copy-start.9
  577.4 2.8 copy-start.9
  594.2 2.8 copy-start.9
  605.3 2.8 copy-start.9
  610.9 2.8 copy-start.9
  622.0 2.8 copy-start.9
  627.6 2.8 copy-start.9
  638.7 2.8 copy-start.9
  (52 other events, 82.2 us)
Sparse Core Ops, SparseCore 0:
  399.7 144.5 all-gather.4
where the time goes:
time: 664 us; the launch traced here: 657 us
  blocking collectives  189 us (28%)
  waiting for transfers between devices  130 us (20%)
  matrix products  119 us (18%)
  local copies, waits for them, and re-layouts  107 us (16%)
  other arithmetic  68.2 us (10%)
  starting transfers between devices  26.7 us (4%)
  between operations  14.3 us (2%)
    all_gather x1, blocking collectives, on_device(): lax.all_gather(key_text, 'ctx', axis=0, tiled=True)  93 us
    all_gather x1, waiting for transfers between devices, combined_all(): pieces = jax.tree.map(lambda part: lax.all_gather(part, axis), value)  92 us
    all_gather x2, blocking collectives, combined_all(): pieces = jax.tree.map(lambda part: lax.all_gather(part, axis), value)  52.6 us
    add x15, other arithmetic, combine_parts(): acc_early * spread_heads(factor_early)  42.2 us
    ppermute x8, waiting for transfers between devices, shifted(): return lax.ppermute(shard, axis, pairs)  38.3 us
    dynamic_slice x45, local copies, waits for them, and re-layouts, combined_all(): lax.scan(lambda total, share: (join(total, share), None), head, tail)  30.1 us
    ppermute x8, starting transfers between devices, shifted(): return lax.ppermute(shard, axis, pairs)  26.7 us
    all_gather x1, blocking collectives, on_device(): lax.all_gather(query_text, 'ctx', axis=0, tiled=True)  24.3 us
  transfers between devices with their start and end apart: 9, of which 3 were waited for; matrix products, arithmetic and copies ran while one was open for 1% of the time, Pallas kernels for 0%

commit v1 on v0

v1 whole, which is shorter than its diff:
```python
import functools
import math

import jax
import jax.numpy as jnp
from jax import lax
from jax.experimental import pallas as pl
from jax.experimental.pallas import tpu as pltpu
from jax.sharding import PartitionSpec as P

TILE = 384
HD = 128
REACH = 2
CHUNK = 3
C2 = math.log2(math.e) / math.sqrt(HD)


def qk(q, k):
    return lax.dot_general(q, k, (((1,), (1,)), ((), ())), preferred_element_type=jnp.float32)


def pv(p, v):
    return lax.dot_general(
        p.astype(jnp.bfloat16), v, (((1,), (0,)), ((), ())), preferred_element_type=jnp.float32
    )


def softmax_parts(scores, values):
    peak = functools.reduce(jnp.maximum, [jnp.max(s, axis=-1, keepdims=True) for s in scores])
    total, acc = None, None
    for s, v in zip(scores, values):
        w = jnp.exp2((s - peak) * C2)
        t = jnp.sum(w, axis=-1, keepdims=True)
        a = pv(w, v)
        total = t if total is None else total + t
        acc = a if acc is None else acc + a
    return peak, total, acc


def video_kernel(meta, q, own, m2, p2, sib, fwd, tk, tv, prev, out):
    lo_p2 = meta[0] == 2
    hi_sib = meta[1] == 3
    hi_fwd = meta[1] == 4
    tiles = []
    for j in range(2):
        far_m, far_p = m2[j], p2[j]
        lo = jnp.where(lo_p2, far_p, far_m)
        hi = jnp.where(hi_fwd, fwd[j], jnp.where(hi_sib, sib[j], far_p))
        tiles.append((own[j], lo, hi))
    key_words = tk[...]
    value_words = tv[...]
    ok = lax.broadcasted_iota(jnp.int32, (1, key_words.shape[0]), 1) < meta[2]
    rows = 128
    for r in range(q.shape[0] // rows):
        qr = q[pl.ds(r * rows, rows), :]
        scores = [qk(qr, k) for k in tiles[0]]
        scores.append(jnp.where(ok, qk(qr, key_words), -jnp.inf))
        _, total, acc = softmax_parts(scores, list(tiles[1]) + [value_words])
        out[pl.ds(r * rows, rows), :] = (acc / total).astype(jnp.bfloat16)


def text_kernel(meta, q, k, v, kt, vt, peak_out, total_out, acc_out):
    h = pl.program_id(0)
    own = kt.shape[0]
    ok = lax.broadcasted_iota(jnp.int32, (1, own), 1) < meta[3]
    scores = [qk(q[...], k[...]), jnp.where(ok, qk(q[...], kt[...]), -jnp.inf)]
    peak, total, acc = softmax_parts(scores, [v[...], vt[...]])
    lane = lax.broadcasted_iota(jnp.int32, peak_out.shape, 1) == h
    peak_out[...] = jnp.where(lane, peak, jnp.where(h == 0, 0.0, peak_out[...]))
    total_out[...] = jnp.where(lane, total, jnp.where(h == 0, 1.0, total_out[...]))
    acc_out[...] = acc


def spread_heads(values, heads):
    return jnp.repeat(values[..., :heads], HD, axis=-1)


def on_device(qv, kv, vv, qt, kt, vt, key_tiles, tile_owner, text_count):
    n = lax.axis_size("ctx")
    me = lax.axis_index("ctx")
    rows, width = qv.shape
    heads = width // HD
    here = qt.shape[0]
    even = me % 2 == 0
    cols = CHUNK * HD
    chunks = heads // CHUNK

    text = lax.all_gather(jnp.stack([qt, kt, vt]), "ctx", axis=1, tiled=True)
    tq, tk, tv = text[0], text[1], text[2]

    tiles = tile_owner.shape[0]
    match = key_tiles[0][:, None] == jnp.arange(tiles, dtype=jnp.int32)[None, :]
    slots = jnp.sum(jnp.where(match, tile_owner[None, :], 0), axis=-1)
    off = slots - me
    near = jnp.where(even == (off == 1), 3, 4)
    code = jnp.where(off == 0, 0, jnp.where(off == -2, 1, jnp.where(off == 2, 2, near)))
    hi = jnp.max(code)
    lo = jnp.sum(code) - hi
    meta = jnp.stack([lo, hi, text_count[0], text_count[0] - me * here]).astype(jnp.int32)

    up = [(i, i - 2) for i in range(2, n)]
    down = [(i, i + 2) for i in range(n - 2)]
    swap = [(i, i ^ 1) for i in range(n)]
    fetched = []
    for c in range(chunks):
        sl = slice(c * cols, (c + 1) * cols)
        own = jnp.stack([kv[:, sl], vv[:, sl]])
        p2 = lax.ppermute(own, "ctx", up)
        m2 = lax.ppermute(own, "ctx", down)
        sib = lax.ppermute(own, "ctx", swap)
        fwd = lax.ppermute(jnp.where(even, p2, m2), "ctx", swap)
        fetched.append((own, m2, p2, sib, fwd))

    col = lambda h: (0, h)
    text_rows = tq.shape[0]
    smem = pl.BlockSpec(memory_space=pltpu.SMEM)
    peak, total, acc = pl.pallas_call(
        text_kernel,
        grid=(heads,),
        in_specs=[
            smem,
            pl.BlockSpec((text_rows, HD), col),
            pl.BlockSpec((rows, HD), col),
            pl.BlockSpec((rows, HD), col),
            pl.BlockSpec((here, HD), col),
            pl.BlockSpec((here, HD), col),
        ],
        out_specs=[
            pl.BlockSpec((text_rows, 128), lambda h: (0, 0)),
            pl.BlockSpec((text_rows, 128), lambda h: (0, 0)),
            pl.BlockSpec((text_rows, HD), col),
        ],
        out_shape=[
            jax.ShapeDtypeStruct((text_rows, 128), jnp.float32),
            jax.ShapeDtypeStruct((text_rows, 128), jnp.float32),
            jax.ShapeDtypeStruct((text_rows, width), jnp.float32),
        ],
        cost_estimate=pl.CostEstimate(
            flops=4 * text_rows * rows * width * 4, bytes_accessed=6 << 20, transcendentals=0
        ),
        name="text_partials",
    )(meta, tq, kv, vv, kt, vt)

    out = jnp.zeros((rows, width), jnp.bfloat16)
    for c in range(chunks):
        own, m2, p2, sib, fwd = fetched[c]
        tile_spec = pl.BlockSpec((2, rows, HD), lambda h: (0, 0, h))
        wide = lambda h, c=c: (0, h + c * CHUNK)
        out = pl.pallas_call(
            video_kernel,
            grid=(CHUNK,),
            in_specs=[smem, pl.BlockSpec((rows, HD), wide)]
            + [tile_spec] * 5
            + [pl.BlockSpec((text_rows, HD), wide)] * 2
            + [pl.BlockSpec(memory_space=pl.ANY)],
            out_specs=pl.BlockSpec((rows, HD), wide),
            out_shape=jax.ShapeDtypeStruct((rows, width), jnp.bfloat16),
            input_output_aliases={9: 0},
            compiler_params=pltpu.CompilerParams(vmem_limit_bytes=32 << 20),
            cost_estimate=pl.CostEstimate(
                flops=4 * rows * (3 * rows + text_rows) * cols * 4,
                bytes_accessed=8 << 20,
                transcendentals=0,
            ),
            name="video_chunk",
        )(meta, qv, own, m2, p2, sib, fwd, tk, tv, out)

    blocks = n
    stats = jnp.stack([peak, total]).reshape(2, blocks, here, 128)
    acc = acc.reshape(blocks, here, width)
    step = 1
    while step < n:
        blocks //= 2
        bit = (me // step) % 2
        pairs = [(i, i ^ step) for i in range(n)]
        stats4 = stats.reshape(2, blocks, 2, here, 128)
        acc4 = acc.reshape(blocks, 2, here, width)
        pick = lambda x, b, ax: jnp.where(
            b == 0, lax.index_in_dim(x, 0, ax, False), lax.index_in_dim(x, 1, ax, False)
        )
        their_s = lax.ppermute(pick(stats4, 1 - bit, 2), "ctx", pairs)
        their_a = lax.ppermute(pick(acc4, 1 - bit, 1), "ctx", pairs)
        my_s = pick(stats4, bit, 2)
        my_a = pick(acc4, bit, 1)
        joint = jnp.maximum(my_s[0], their_s[0])
        f_my = jnp.exp2((my_s[0] - joint) * C2)
        f_their = jnp.exp2((their_s[0] - joint) * C2)
        stats = jnp.stack([joint, my_s[1] * f_my + their_s[1] * f_their])
        acc = my_a * spread_heads(f_my, heads) + their_a * spread_heads(f_their, heads)
        step *= 2
    text_out = (acc[0] / spread_heads(stats[1, 0], heads)).astype(jnp.bfloat16)
    return (out, text_out)


def solution(mesh):
    split = P(("groups", "ctx"), None)
    return jax.shard_map(
        on_device,
        mesh=mesh,
        in_specs=(split,) * 7 + (P("groups"), P("groups")),
        out_specs=(split, split),
        check_vma=False,
    )
```

time: 664 us -> 220 us (0.33)
  the two profiles are of different devices: /device:TPU:15 before, /device:TPU:0 now
where the time goes in v1:
time: 220 us; the launch traced here: 219 us
  waiting for transfers between devices  94.6 us (43%)
  starting transfers between devices  40.9 us (19%)
  Pallas kernels  37 us (17%)
  between operations  16.6 us (8%)
  other arithmetic  16.1 us (7%)
  local copies, waits for them, and re-layouts  13.3 us (6%)
    ppermute x4, waiting for transfers between devices, on_device(): m2 = lax.ppermute(own, 'ctx', down)  76.9 us
    pallas_call x4, Pallas kernels, on_device(): pl.pallas_call(video_kernel, grid=(CHUNK,), in_specs=[smem, pl.BlockSpec(...  26.1 us
    ppermute x4, starting transfers between devices, on_device(): m2 = lax.ppermute(own, 'ctx', down)  20.9 us
    ppermute x4, waiting for transfers between devices, on_device(): their_a = lax.ppermute(pick(acc4, 1 - bit, 1), 'ctx', pairs)  16.8 us
    pallas_call x1, Pallas kernels, on_device(): pl.pallas_call(text_kernel, grid=(heads,), in_specs=[smem, pl.BlockSpec((...  10.9 us
    ppermute x4, starting transfers between devices, on_device(): their_s = lax.ppermute(pick(stats4, 1 - bit, 2), 'ctx', pairs)  8.21 us
    select_n x4, other arithmetic, on_device(): fwd = lax.ppermute(jnp.where(even, p2, m2), 'ctx', swap)  6.82 us
    ppermute x4, starting transfers between devices, on_device(): p2 = lax.ppermute(own, 'ctx', up)  5.12 us
  transfers between devices with their start and end apart: 25, of which 8 were waited for; matrix products, arithmetic and copies ran while one was open for 11% of the time, Pallas kernels for 17%

profile of v1, /device:TPU:0, one launch (start us, length us, event | category | flops | bytes accessed | tf_op | source)
XLA Modules:
  0.0 218.6 jit_solution(13315407556115778942)
XLA Ops:
  7.2 1.5 pad_maximum_fusion.4
  8.8 1.9 slice_bitcast_fusion.7
  10.7 5.7 %collective-permute-start.12 = (bf16[2,384,384]{2,1,0:T(8,128)(2,1)S(1)}, bf16[2,384,384]{2,1,0:T(8,128)(2,1)}, u32[]{:S(2)}, u32[]{:S(2)}) collective-permute-start(bf16[2,384,384]{2,1,0:T(8,128)(2,1)S(1)} %pad_maximum_fusion.3.own), channel_id=1, source_target_pairs={{0,2},{1,3},{2,4},{3,5},{4,6},{5,7},{6,8},{7,9},{8,10},{9,11},{10,... | collective-permute-start | bytes 1769480 | tf_op jit(solution)/shard_map/ppermute | solution.py:109
  16.4 1.3 collective-permute-start.13
  17.8 5.4 %collective-permute-start.8 = (bf16[2,384,384]{2,1,0:T(8,128)(2,1)S(1)}, bf16[2,384,384]{2,1,0:T(8,128)(2,1)}, u32[]{:S(2)}, u32[]{:S(2)}) collective-permute-start(bf16[2,384,384]{2,1,0:T(8,128)(2,1)S(1)} %pad_maximum_fusion.2.own), channel_id=1, source_target_pairs={{0,2},{1,3},{2,4},{3,5},{4,6},{5,7},{6,8},{7,9},{8,10},{9,11},{10,... | collective-permute-start | bytes 1769480 | tf_op jit(solution)/shard_map/ppermute | solution.py:109
  23.2 1.3 collective-permute-start.9
  24.6 4.6 %collective-permute-start.4 = (bf16[2,384,384]{2,1,0:T(8,128)(2,1)S(1)}, bf16[2,384,384]{2,1,0:T(8,128)(2,1)S(1)}, u32[]{:S(2)}, u32[]{:S(2)}) collective-permute-start(bf16[2,384,384]{2,1,0:T(8,128)(2,1)S(1)} %pad_maximum_fusion.1.own), channel_id=1, source_target_pairs={{0,2},{1,3},{2,4},{3,5},{4,6},{5,7},{6,8},{7,9},{8,10},{9,11},{10,... | collective-permute-start | bytes 1769480 | tf_op jit(solution)/shard_map/ppermute | solution.py:109
  29.8 0.2 select_reduce_fusion
  30.0 0.7 fusion.57
  32.2 24.0 %collective-permute-done.12.m2 = bf16[2,384,384]{2,1,0:T(8,128)(2,1)} collective-permute-done((bf16[2,384,384]{2,1,0:T(8,128)(2,1)S(1)}, bf16[2,384,384]{2,1,0:T(8,128)(2,1)}, u32[]{:S(2)}, u32[]{:S(2)}) %collective-permute-start.12) | collective-permute-done | bytes 589856 | tf_op jit(solution)/shard_map/ppermute | solution.py:109
  56.1 1.3 collective-permute-start.5
  57.4 1.3 pad_add_fusion.meta
  58.7 5.1 %collective-permute-start = (bf16[2,384,384]{2,1,0:T(8,128)(2,1)S(1)}, bf16[2,384,384]{2,1,0:T(8,128)(2,1)S(1)}, u32[]{:S(2)}, u32[]{:S(2)}) collective-permute-start(bf16[2,384,384]{2,1,0:T(8,128)(2,1)S(1)} %pad_maximum_fusion.own), channel_id=1, source_target_pairs={{0,2},{1,3},{2,4},{3,5},{4,6},{5,7},{6,8},{7,9},{8,10},{9,11},{10,... | collective-permute-start | bytes 1769480 | tf_op jit(solution)/shard_map/ppermute | solution.py:109
  63.9 23.9 %collective-permute-done.8.m2 = bf16[2,384,384]{2,1,0:T(8,128)(2,1)} collective-permute-done((bf16[2,384,384]{2,1,0:T(8,128)(2,1)S(1)}, bf16[2,384,384]{2,1,0:T(8,128)(2,1)}, u32[]{:S(2)}, u32[]{:S(2)}) %collective-permute-start.8) | collective-permute-done | bytes 589856 | tf_op jit(solution)/shard_map/ppermute | solution.py:109
  87.7 1.3 collective-permute-start.1
  89.0 2.0 broadcast_select_fusion
  91.0 2.0 broadcast_select_fusion.1
  93.0 20.0 %collective-permute-done.4.m2 = bf16[2,384,384]{2,1,0:T(8,128)(2,1)S(1)} collective-permute-done((bf16[2,384,384]{2,1,0:T(8,128)(2,1)S(1)}, bf16[2,384,384]{2,1,0:T(8,128)(2,1)S(1)}, u32[]{:S(2)}, u32[]{:S(2)}) %collective-permute-start.4) | collective-permute-done | bytes 589856 | tf_op jit(solution)/shard_map/ppermute | solution.py:109
  113.0 0.5 collective-permute-start.6
  113.5 2.0 broadcast_select_fusion.2
  115.5 9.0 %collective-permute-done.m2 = bf16[2,384,384]{2,1,0:T(8,128)(2,1)S(1)} collective-permute-done((bf16[2,384,384]{2,1,0:T(8,128)(2,1)S(1)}, bf16[2,384,384]{2,1,0:T(8,128)(2,1)S(1)}, u32[]{:S(2)}, u32[]{:S(2)}) %collective-permute-start) | collective-permute-done | bytes 589856 | tf_op jit(solution)/shard_map/ppermute | solution.py:109
  124.5 0.5 collective-permute-start.11
  125.0 0.9 broadcast_select_fusion.3
  125.9 0.8 copy-done.4
  126.8 0.9 copy-done.6
  127.6 2.6 %slice_bitcast_fusion.2 = (bf16[256,1536]{1,0:T(8,128)(2,1)}, bf16[256,1536]{1,0:T(8,128)(2,1)S(1)}, bf16[256,1536]{1,0:T(8,128)(2,1)S(1)}) fusion(bf16[3,256,1536]{2,1,0:T(8,128)(2,1)} %all-gather.2.cloned.1.call-done), kind=kLoop, calls=%fused_computation.2 | loop fusion | bytes 4718592 | tf_op jit(solution)/shard_map/squeeze | solution.py:89
  130.3 10.9 %text_partials.1 = (f32[256,128]{1,0:T(8,128)}, f32[256,128]{1,0:T(8,128)}, f32[256,1536]{1,0:T(8,128)}) custom-call(s32[4]{0:T(128)} %pad_add_fusion.meta, bf16[256,1536]{1,0:T(8,128)(2,1)} %get-tuple-element.16.q, bf16[384,1536]{1,0:T(8,128)(2,1)} %k.1, bf16[384,1536]{1,0:T(8,128)(2,1)} %v.1, bf16[16,1536]{1,0:T(8,128)(2,1)} %kt.1, bf16[16,1536]{1,0:T(8,128)(2,1)} %vt.1), custom_call_target="tpu_custom_call" | custom-call | flops 2415919104 | bytes 6291456 | tf_op jit(solution)/shard_map/text_partials/pallas_call | solution.py:117
  141.2 2.5 %select_bitcast_fusion = f32[8,16,1536]{2,1,0:T(8,128)} fusion(f32[8,2,16,1536]{3,2,1,0:T(8,128)} %bitcast.256, pred[]{:T(512)S(6)} %eq.86), kind=kLoop, calls=%fused_computation.7 | loop fusion | flops 196608 | bytes 2359297 | tf_op jit(solution)/shard_map/jit(_where)/select_n | solution.py:178
  143.8 0.5 collective-permute-start.7
  144.3 1.1 broadcast_in_dim.67.prev
  145.4 6.7 %video_chunk.4.prev = bf16[384,1536]{1,0:T(8,128)(2,1)} custom-call(s32[4]{0:T(128)S(1)} %copy-done.8, bf16[384,1536]{1,0:T(8,128)(2,1)S(1)} %copy-done.9, bf16[2,384,384]{2,1,0:T(8,128)(2,1)S(1)} %pad_maximum_fusion.3.own, bf16[2,384,384]{2,1,0:T(8,128)(2,1)} %collective-permute-done.12.m2, ...), custom_call_target="tpu_custom_call", output_to_operand_aliasing={{}: (9, {})} | custom-call | flops 3321888768 | bytes 8388608 | tf_op jit(solution)/shard_map/video_chunk/pallas_call | solution.py:149
  152.1 0.1 collective-permute-start.3
  152.2 0.4 collective-permute-start.16
  152.7 6.6 %video_chunk.5.prev = bf16[384,1536]{1,0:T(8,128)(2,1)} custom-call(s32[4]{0:T(128)S(1)} %copy-done.8, bf16[384,1536]{1,0:T(8,128)(2,1)S(1)} %copy-done.9, bf16[2,384,384]{2,1,0:T(8,128)(2,1)S(1)} %pad_maximum_fusion.2.own, bf16[2,384,384]{2,1,0:T(8,128)(2,1)} %collective-permute-done.8.m2, ...), custom_call_target="tpu_custom_call", output_to_operand_aliasing={{}: (9, {})} | custom-call | flops 3321888768 | bytes 8388608 | tf_op jit(solution)/shard_map/video_chunk/pallas_call | solution.py:149
  159.3 0.2 collective-permute-start.17
  159.5 6.6 %video_chunk.6.prev = bf16[384,1536]{1,0:T(8,128)(2,1)} custom-call(s32[4]{0:T(128)S(1)} %copy-done.8, bf16[384,1536]{1,0:T(8,128)(2,1)S(1)} %copy-done.9, bf16[2,384,384]{2,1,0:T(8,128)(2,1)S(1)} %pad_maximum_fusion.1.own, bf16[2,384,384]{2,1,0:T(8,128)(2,1)S(1)} %copy-done.3, ...), custom_call_target="tpu_custom_call", output_to_operand_aliasing={{}: (9, {})} | custom-call | flops 3321888768 | bytes 8388608 | tf_op jit(solution)/shard_map/video_chunk/pallas_call | solution.py:149
  166.1 6.3 %video_chunk.7 = bf16[384,1536]{1,0:T(8,128)(2,1)} custom-call(s32[4]{0:T(128)S(1)} %copy-done.8, bf16[384,1536]{1,0:T(8,128)(2,1)S(1)} %copy-done.9, bf16[2,384,384]{2,1,0:T(8,128)(2,1)S(1)} %copy-done.1, bf16[2,384,384]{2,1,0:T(8,128)(2,1)S(1)} %copy-done.5, bf16[2,384,384]{2,1,0:T(8,128)(2,1)S(1)} %copy-done.7, ...), custom_call_target="tpu_custom_call", output_to_operand_aliasing={{}: (9, {})} | custom-call | flops 3321888768 | bytes 8388608 | tf_op jit(solution)/shard_map/video_chunk/pallas_call | solution.py:149
  172.4 2.6 %collective-permute-start.18 = (f32[2,4,16,128]{3,2,1,0:T(8,128)S(1)}, f32[2,4,16,128]{3,2,1,0:T(8,128)S(1)}, u32[]{:S(2)}, u32[]{:S(2)}) collective-permute-start(f32[2,4,16,128]{3,2,1,0:T(8,128)S(1)} %select_bitcast_fusion.5), channel_id=1, source_target_pairs={{0,2},{1,3},{2,0},{3,1},{4,6},{5,7},{6,4},{7,5},{8,10},{9,11},{10,... | collective-permute-start | bytes 196616 | tf_op jit(solution)/shard_map/ppermute | solution.py:181
  175.1 0.3 broadcast_in_dim.68
  175.4 1.0 reshape.282
  176.5 0.3 broadcast_in_dim.69
  176.8 1.0 reshape.283
  177.9 2.3 %collective-permute-start.20 = (f32[2,2,16,128]{3,2,1,0:T(8,128)S(1)}, f32[2,2,16,128]{3,2,1,0:T(8,128)S(1)}, u32[]{:S(2)}, u32[]{:S(2)}) collective-permute-start(f32[2,2,16,128]{3,2,1,0:T(8,128)S(1)} %select_bitcast_fusion.6), channel_id=1, source_target_pairs={{0,4},{1,5},{2,6},{3,7},{4,0},{5,1},{6,2},{7,3},{8,12},{9,13},{10,... | collective-permute-start | bytes 98312 | tf_op jit(solution)/shard_map/ppermute | solution.py:181
  180.2 0.2 broadcast_in_dim.70
  180.4 0.8 reshape.285
  181.3 0.2 broadcast_in_dim.71
  181.5 0.8 reshape.286
  182.3 2.9 %collective-permute-start.22 = (f32[2,1,16,128]{3,2,0,1:T(8,128)S(1)}, f32[2,1,16,128]{3,2,0,1:T(8,128)S(1)}, u32[]{:S(2)}, u32[]{:S(2)}) collective-permute-start(f32[2,1,16,128]{3,2,0,1:T(8,128)S(1)} %fusion.37), channel_id=1, source_target_pairs={{0,8},{1,9},{2,10},{3,11},{4,12},{5,13},{6,14},{7,15},{8,0},{9,1},... | collective-permute-start | bytes 49160 | tf_op jit(solution)/shard_map/ppermute | solution.py:181
  185.3 0.6 slice_bitcast_fusion.29
  185.9 0.1 broadcast_in_dim.72
  186.0 0.1 broadcast_in_dim.73
  186.2 0.8 collective-permute-done.22
  187.1 1.7 fusion
  188.8 1.2 collective-permute-start.19
  190.0 7.8 %collective-permute-done.19 = f32[4,16,1536]{2,1,0:T(8,128)S(1)} collective-permute-done((f32[4,16,1536]{2,1,0:T(8,128)S(1)}, f32[4,16,1536]{2,1,0:T(8,128)S(1)}, u32[]{:S(2)}, u32[]{:S(2)}) %collective-permute-start.19) | collective-permute-done | bytes 393248 | tf_op jit(solution)/shard_map/ppermute | solution.py:182
  197.9 0.1 fusion.1
  198.0 1.0 collective-permute-start.21
  199.1 5.2 %collective-permute-done.21 = f32[2,16,1536]{2,1,0:T(8,128)S(1)} collective-permute-done((f32[2,16,1536]{2,1,0:T(8,128)S(1)}, f32[2,16,1536]{2,1,0:T(8,128)S(1)}, u32[]{:S(2)}, u32[]{:S(2)}) %collective-permute-start.21) | collective-permute-done | bytes 196640 | tf_op jit(solution)/shard_map/ppermute | solution.py:182
  204.3 2.6 %collective-permute-start.23 = (f32[1,16,1536]{2,1,0:T(8,128)S(1)}, f32[1,16,1536]{2,1,0:T(8,128)S(1)}, u32[]{:S(2)}, u32[]{:S(2)}) collective-permute-start(f32[1,16,1536]{2,1,0:T(8,128)S(1)} %select_bitcast_fusion.4), channel_id=1, source_target_pairs={{0,8},{1,9},{2,10},{3,11},{4,12},{5,13},{6,14},{7,15},{8,0},{9,1},... | collective-permute-start | bytes 294920 | tf_op jit(solution)/shard_map/ppermute | solution.py:182
  206.9 0.1 broadcast_in_dim.74
  207.0 0.1 broadcast_in_dim.76
  207.2 3.8 %collective-permute-done.23 = f32[1,16,1536]{2,1,0:T(8,128)S(1)} collective-permute-done((f32[1,16,1536]{2,1,0:T(8,128)S(1)}, f32[1,16,1536]{2,1,0:T(8,128)S(1)}, u32[]{:S(2)}, u32[]{:S(2)}) %collective-permute-start.23) | collective-permute-done | bytes 98336 | tf_op jit(solution)/shard_map/ppermute | solution.py:182
  211.0 0.1 broadcast_in_dim.78
  211.1 0.7 fusion.9
  (104 shorter events, 1.1 us)
Async XLA Ops:
  7.2 120.5 %all-gather.2.cloned.1.call-start = ((), (), s32[]{:S(2)}) async-start(), calls=%async_computation | async-start | bytes 2506752 | tf_op jit(solution)/shard_map/all_gather | solution.py:88
  10.7 45.5 %collective-permute-start.12 = (bf16[2,384,384]{2,1,0:T(8,128)(2,1)S(1)}, bf16[2,384,384]{2,1,0:T(8,128)(2,1)}, u32[]{:S(2)}, u32[]{:S(2)}) collective-permute-start(bf16[2,384,384]{2,1,0:T(8,128)(2,1)S(1)} %pad_maximum_fusion.3.own), channel_id=1, source_target_pairs={{0,2},{1,3},{2,4},{3,5},{4,6},{5,7},{6,8},{7,9},{8,10},{9,11},{10,... | collective-permute-start | bytes 1769480 | tf_op jit(solution)/shard_map/ppermute | solution.py:109
  16.4 42.3 %collective-permute-start.13 = (bf16[2,384,384]{2,1,0:T(8,128)(2,1)S(1)}, bf16[2,384,384]{2,1,0:T(8,128)(2,1)}, u32[]{:S(2)}, u32[]{:S(2)}) collective-permute-start(bf16[2,384,384]{2,1,0:T(8,128)(2,1)S(1)} %pad_maximum_fusion.3.own), channel_id=1, source_target_pairs={{2,0},{3,1},{4,2},{5,3},{6,4},{7,5},{8,6},{9,7},{10,8},{11,9},{12,... | collective-permute-start | bytes 1769480 | tf_op jit(solution)/shard_map/ppermute | solution.py:108
  17.7 12.1 %copy-start.21 = (s32[16]{0:T(128)S(1)}, s32[16]{0:T(128)}, u32[]{:S(2)}) copy-start(s32[16]{0:T(128)} %param.16) | copy-start | bytes 196
  17.7 12.1 %copy-start.22 = (s32[1,3]{1,0:T(1,128)S(1)}, s32[1,3]{1,0:T(1,128)}, u32[]{:S(2)}) copy-start(s32[1,3]{1,0:T(1,128)} %param.15) | copy-start | bytes 40
  17.8 69.9 %collective-permute-start.8 = (bf16[2,384,384]{2,1,0:T(8,128)(2,1)S(1)}, bf16[2,384,384]{2,1,0:T(8,128)(2,1)}, u32[]{:S(2)}, u32[]{:S(2)}) collective-permute-start(bf16[2,384,384]{2,1,0:T(8,128)(2,1)S(1)} %pad_maximum_fusion.2.own), channel_id=1, source_target_pairs={{0,2},{1,3},{2,4},{3,5},{4,6},{5,7},{6,8},{7,9},{8,10},{9,11},{10,... | collective-permute-start | bytes 1769480 | tf_op jit(solution)/shard_map/ppermute | solution.py:109
  23.2 67.8 %collective-permute-start.9 = (bf16[2,384,384]{2,1,0:T(8,128)(2,1)S(1)}, bf16[2,384,384]{2,1,0:T(8,128)(2,1)}, u32[]{:S(2)}, u32[]{:S(2)}) collective-permute-start(bf16[2,384,384]{2,1,0:T(8,128)(2,1)S(1)} %pad_maximum_fusion.2.own), channel_id=1, source_target_pairs={{2,0},{3,1},{4,2},{5,3},{6,4},{7,5},{8,6},{9,7},{10,8},{11,9},{12,... | collective-permute-start | bytes 1769480 | tf_op jit(solution)/shard_map/ppermute | solution.py:108
  24.6 88.5 %collective-permute-start.4 = (bf16[2,384,384]{2,1,0:T(8,128)(2,1)S(1)}, bf16[2,384,384]{2,1,0:T(8,128)(2,1)S(1)}, u32[]{:S(2)}, u32[]{:S(2)}) collective-permute-start(bf16[2,384,384]{2,1,0:T(8,128)(2,1)S(1)} %pad_maximum_fusion.1.own), channel_id=1, source_target_pairs={{0,2},{1,3},{2,4},{3,5},{4,6},{5,7},{6,8},{7,9},{8,10},{9,11},{10,... | collective-permute-start | bytes 1769480 | tf_op jit(solution)/shard_map/ppermute | solution.py:109
  32.2 60.8 %copy-start = (bf16[2,384,384]{2,1,0:T(8,128)(2,1)}, bf16[2,384,384]{2,1,0:T(8,128)(2,1)S(1)}, u32[]{:S(2)}) copy-start(bf16[2,384,384]{2,1,0:T(8,128)(2,1)S(1)} %pad_maximum_fusion.own) | copy-start | bytes 1769476
  56.1 56.9 %collective-permute-start.5 = (bf16[2,384,384]{2,1,0:T(8,128)(2,1)S(1)}, bf16[2,384,384]{2,1,0:T(8,128)(2,1)}, u32[]{:S(2)}, u32[]{:S(2)}) collective-permute-start(bf16[2,384,384]{2,1,0:T(8,128)(2,1)S(1)} %pad_maximum_fusion.1.own), channel_id=1, source_target_pairs={{2,0},{3,1},{4,2},{5,3},{6,4},{7,5},{8,6},{9,7},{10,8},{11,9},{12,... | collective-permute-start | bytes 1769480 | tf_op jit(solution)/shard_map/ppermute | solution.py:108
  58.7 65.8 %collective-permute-start = (bf16[2,384,384]{2,1,0:T(8,128)(2,1)S(1)}, bf16[2,384,384]{2,1,0:T(8,128)(2,1)S(1)}, u32[]{:S(2)}, u32[]{:S(2)}) collective-permute-start(bf16[2,384,384]{2,1,0:T(8,128)(2,1)S(1)} %pad_maximum_fusion.own), channel_id=1, source_target_pairs={{0,2},{1,3},{2,4},{3,5},{4,6},{5,7},{6,8},{7,9},{8,10},{9,11},{10,... | collective-permute-start | bytes 1769480 | tf_op jit(solution)/shard_map/ppermute | solution.py:109
  87.7 36.8 %collective-permute-start.1 = (bf16[2,384,384]{2,1,0:T(8,128)(2,1)S(1)}, bf16[2,384,384]{2,1,0:T(8,128)(2,1)S(1)}, u32[]{:S(2)}, u32[]{:S(2)}) collective-permute-start(bf16[2,384,384]{2,1,0:T(8,128)(2,1)S(1)} %pad_maximum_fusion.own), channel_id=1, source_target_pairs={{2,0},{3,1},{4,2},{5,3},{6,4},{7,5},{8,6},{9,7},{10,8},{11,9},{12,... | collective-permute-start | bytes 1769480 | tf_op jit(solution)/shard_map/ppermute | solution.py:108
  91.0 52.7 %collective-permute-start.14 = (bf16[2,384,384]{2,1,0:T(8,128)(2,1)S(1)}, bf16[2,384,384]{2,1,0:T(8,128)(2,1)}, u32[]{:S(2)}, u32[]{:S(2)}) collective-permute-start(bf16[2,384,384]{2,1,0:T(8,128)(2,1)S(1)} %pad_maximum_fusion.3.own), channel_id=1, source_target_pairs={{0,1},{1,0},{2,3},{3,2},{4,5},{5,4},{6,7},{7,6},{8,9},{9,8},{10,11... | collective-permute-start | bytes 1769480 | tf_op jit(solution)/shard_map/ppermute | solution.py:110
  113.0 12.9 %copy-start.2 = (bf16[2,384,384]{2,1,0:T(8,128)(2,1)}, bf16[2,384,384]{2,1,0:T(8,128)(2,1)S(1)}, u32[]{:S(2)}) copy-start(bf16[2,384,384]{2,1,0:T(8,128)(2,1)S(1)} %collective-permute-done.4.m2) | copy-start | bytes 1769476
  113.0 39.1 %collective-permute-start.10 = (bf16[2,384,384]{2,1,0:T(8,128)(2,1)S(1)}, bf16[2,384,384]{2,1,0:T(8,128)(2,1)}, u32[]{:S(2)}, u32[]{:S(2)}) collective-permute-start(bf16[2,384,384]{2,1,0:T(8,128)(2,1)S(1)} %pad_maximum_fusion.2.own), channel_id=1, source_target_pairs={{0,1},{1,0},{2,3},{3,2},{4,5},{5,4},{6,7},{7,6},{8,9},{9,8},{10,11... | collective-permute-start | bytes 1769480 | tf_op jit(solution)/shard_map/ppermute | solution.py:110
  113.0 46.3 %collective-permute-start.6 = (bf16[2,384,384]{2,1,0:T(8,128)(2,1)S(1)}, bf16[2,384,384]{2,1,0:T(8,128)(2,1)}, u32[]{:S(2)}, u32[]{:S(2)}) collective-permute-start(bf16[2,384,384]{2,1,0:T(8,128)(2,1)S(1)} %pad_maximum_fusion.1.own), channel_id=1, source_target_pairs={{0,1},{1,0},{2,3},{3,2},{4,5},{5,4},{6,7},{7,6},{8,9},{9,8},{10,11... | collective-permute-start | bytes 1769480 | tf_op jit(solution)/shard_map/ppermute | solution.py:110
  124.5 19.3 %collective-permute-start.15 = (bf16[2,384,384]{2,1,0:T(8,128)(2,1)}, bf16[2,384,384]{2,1,0:T(8,128)(2,1)}, u32[]{:S(2)}, u32[]{:S(2)}) collective-permute-start(bf16[2,384,384]{2,1,0:T(8,128)(2,1)} %broadcast_select_fusion), channel_id=1, source_target_pairs={{0,1},{1,0},{2,3},{3,2},{4,5},{5,4},{6,7},{7,6},{8,9},{9,8},{10,11... | collective-permute-start | bytes 1769480 | tf_op jit(solution)/shard_map/ppermute | solution.py:111
  124.5 27.7 %collective-permute-start.11 = (bf16[2,384,384]{2,1,0:T(8,128)(2,1)}, bf16[2,384,384]{2,1,0:T(8,128)(2,1)}, u32[]{:S(2)}, u32[]{:S(2)}) collective-permute-start(bf16[2,384,384]{2,1,0:T(8,128)(2,1)} %broadcast_select_fusion.1), channel_id=1, source_target_pairs={{0,1},{1,0},{2,3},{3,2},{4,5},{5,4},{6,7},{7,6},{8,9},{9,8},{10,11... | collective-permute-start | bytes 1769480 | tf_op jit(solution)/shard_map/ppermute | solution.py:111
  125.9 0.8 copy-start.4
  126.8 0.9 copy-start.6
  141.2 2.5 %copy-start.16 = (f32[256,128]{1,0:T(8,128)S(1)}, f32[256,128]{1,0:T(8,128)}, u32[]{:S(2)}) copy-start(f32[256,128]{1,0:T(8,128)} %get-tuple-element.6) | copy-start | bytes 393220
  141.2 2.5 %copy-start.17 = (f32[256,128]{1,0:T(8,128)S(1)}, f32[256,128]{1,0:T(8,128)}, u32[]{:S(2)}) copy-start(f32[256,128]{1,0:T(8,128)} %get-tuple-element.7) | copy-start | bytes 393220
  141.2 2.5 %copy-start.1 = (bf16[2,384,384]{2,1,0:T(8,128)(2,1)S(1)}, bf16[2,384,384]{2,1,0:T(8,128)(2,1)}, u32[]{:S(2)}) copy-start(bf16[2,384,384]{2,1,0:T(8,128)(2,1)} %copy-done) | copy-start | bytes 1769476
  141.2 2.6 %copy-start.14 = (bf16[2,384,384]{2,1,0:T(8,128)(2,1)S(1)}, bf16[2,384,384]{2,1,0:T(8,128)(2,1)}, u32[]{:S(2)}) copy-start(bf16[2,384,384]{2,1,0:T(8,128)(2,1)} %broadcast_select_fusion.2) | copy-start | bytes 1769476
  143.7 1.7 copy-start.8
  143.7 1.7 copy-start.9
  143.7 22.3 %collective-permute-start.2 = (bf16[2,384,384]{2,1,0:T(8,128)(2,1)S(1)}, bf16[2,384,384]{2,1,0:T(8,128)(2,1)S(1)}, u32[]{:S(2)}, u32[]{:S(2)}) collective-permute-start(bf16[2,384,384]{2,1,0:T(8,128)(2,1)S(1)} %copy-done.1), channel_id=1, source_target_pairs={{0,1},{1,0},{2,3},{3,2},{4,5},{5,4},{6,7},{7,6},{8,9},{9,8},{10,11... | collective-permute-start | bytes 1769480 | tf_op jit(solution)/shard_map/ppermute | solution.py:110
  143.8 15.7 %collective-permute-start.7 = (bf16[2,384,384]{2,1,0:T(8,128)(2,1)S(1)}, bf16[2,384,384]{2,1,0:T(8,128)(2,1)S(1)}, u32[]{:S(2)}, u32[]{:S(2)}) collective-permute-start(bf16[2,384,384]{2,1,0:T(8,128)(2,1)S(1)} %copy-done.14), channel_id=1, source_target_pairs={{0,1},{1,0},{2,3},{3,2},{4,5},{5,4},{6,7},{7,6},{8,9},{9,8},{10,11... | collective-permute-start | bytes 1769480 | tf_op jit(solution)/shard_map/ppermute | solution.py:111
  145.4 6.7 %copy-start.15 = (bf16[2,384,384]{2,1,0:T(8,128)(2,1)S(1)}, bf16[2,384,384]{2,1,0:T(8,128)(2,1)}, u32[]{:S(2)}) copy-start(bf16[2,384,384]{2,1,0:T(8,128)(2,1)} %broadcast_select_fusion.3) | copy-start | bytes 1769476
  152.1 14.0 %collective-permute-start.3 = (bf16[2,384,384]{2,1,0:T(8,128)(2,1)S(1)}, bf16[2,384,384]{2,1,0:T(8,128)(2,1)S(1)}, u32[]{:S(2)}, u32[]{:S(2)}) collective-permute-start(bf16[2,384,384]{2,1,0:T(8,128)(2,1)S(1)} %copy-done.15), channel_id=1, source_target_pairs={{0,1},{1,0},{2,3},{3,2},{4,5},{5,4},{6,7},{7,6},{8,9},{9,8},{10,11... | collective-permute-start | bytes 1769480 | tf_op jit(solution)/shard_map/ppermute | solution.py:111
  152.2 7.3 %copy-start.3 = (bf16[2,384,384]{2,1,0:T(8,128)(2,1)S(1)}, bf16[2,384,384]{2,1,0:T(8,128)(2,1)}, u32[]{:S(2)}) copy-start(bf16[2,384,384]{2,1,0:T(8,128)(2,1)} %copy-done.2) | copy-start | bytes 1769476
  152.2 20.1 %collective-permute-start.16 = (f32[2,8,16,128]{3,2,1,0:T(8,128)S(1)}, f32[2,8,16,128]{3,2,1,0:T(8,128)S(1)}, u32[]{:S(2)}, u32[]{:S(2)}) collective-permute-start(f32[2,8,16,128]{3,2,1,0:T(8,128)S(1)} %get-tuple-element.28), channel_id=1, source_target_pairs={{0,1},{1,0},{2,3},{3,2},{4,5},{5,4},{6,7},{7,6},{8,9},{9,8},{10,11... | collective-permute-start | bytes 393224 | tf_op jit(solution)/shard_map/ppermute | solution.py:181
  159.3 6.8 %copy-start.5 = (bf16[2,384,384]{2,1,0:T(8,128)(2,1)S(1)}, bf16[2,384,384]{2,1,0:T(8,128)(2,1)}, u32[]{:S(2)}) copy-start(bf16[2,384,384]{2,1,0:T(8,128)(2,1)} %copy-done.4) | copy-start | bytes 1769476
  159.3 6.8 %copy-start.7 = (bf16[2,384,384]{2,1,0:T(8,128)(2,1)S(1)}, bf16[2,384,384]{2,1,0:T(8,128)(2,1)}, u32[]{:S(2)}) copy-start(bf16[2,384,384]{2,1,0:T(8,128)(2,1)} %copy-done.6) | copy-start | bytes 1769476
  159.3 27.7 %collective-permute-start.17 = (f32[8,16,1536]{2,1,0:T(8,128)}, f32[8,16,1536]{2,1,0:T(8,128)}, u32[]{:S(2)}, u32[]{:S(2)}) collective-permute-start(f32[8,16,1536]{2,1,0:T(8,128)} %select_bitcast_fusion), channel_id=1, source_target_pairs={{0,1},{1,0},{2,3},{3,2},{4,5},{5,4},{6,7},{7,6},{8,9},{9,8},{10,11... | collective-permute-start | bytes 2359304 | tf_op jit(solution)/shard_map/ppermute | solution.py:182
  172.4 5.4 %collective-permute-start.18 = (f32[2,4,16,128]{3,2,1,0:T(8,128)S(1)}, f32[2,4,16,128]{3,2,1,0:T(8,128)S(1)}, u32[]{:S(2)}, u32[]{:S(2)}) collective-permute-start(f32[2,4,16,128]{3,2,1,0:T(8,128)S(1)} %select_bitcast_fusion.5), channel_id=1, source_target_pairs={{0,2},{1,3},{2,0},{3,1},{4,6},{5,7},{6,4},{7,5},{8,10},{9,11},{10,... | collective-permute-start | bytes 196616 | tf_op jit(solution)/shard_map/ppermute | solution.py:181
  177.9 4.4 %collective-permute-start.20 = (f32[2,2,16,128]{3,2,1,0:T(8,128)S(1)}, f32[2,2,16,128]{3,2,1,0:T(8,128)S(1)}, u32[]{:S(2)}, u32[]{:S(2)}) collective-permute-start(f32[2,2,16,128]{3,2,1,0:T(8,128)S(1)} %select_bitcast_fusion.6), channel_id=1, source_target_pairs={{0,4},{1,5},{2,6},{3,7},{4,0},{5,1},{6,2},{7,3},{8,12},{9,13},{10,... | collective-permute-start | bytes 98312 | tf_op jit(solution)/shard_map/ppermute | solution.py:181
  181.5 5.6 %copy-start.11 = (f32[8,16,1536]{2,1,0:T(8,128)S(1)}, f32[8,16,1536]{2,1,0:T(8,128)}, u32[]{:S(2)}) copy-start(f32[8,16,1536]{2,1,0:T(8,128)} %reshape.282) | copy-start | bytes 2359300
  182.3 4.8 %copy-start.10 = (f32[256,1536]{1,0:T(8,128)S(1)}, f32[256,1536]{1,0:T(8,128)}, u32[]{:S(2)}) copy-start(f32[256,1536]{1,0:T(8,128)} %get-tuple-element.5) | copy-start | bytes 4718596
  182.3 4.7 %collective-permute-start.22 = (f32[2,1,16,128]{3,2,0,1:T(8,128)S(1)}, f32[2,1,16,128]{3,2,0,1:T(8,128)S(1)}, u32[]{:S(2)}, u32[]{:S(2)}) collective-permute-start(f32[2,1,16,128]{3,2,0,1:T(8,128)S(1)} %fusion.37), channel_id=1, source_target_pairs={{0,8},{1,9},{2,10},{3,11},{4,12},{5,13},{6,14},{7,15},{8,0},{9,1},... | collective-permute-start | bytes 49160 | tf_op jit(solution)/shard_map/ppermute | solution.py:181
  188.7 1.3 copy-start.20
  188.8 9.1 %copy-start.12 = (f32[4,16,1536]{2,1,0:T(8,128)S(1)}, f32[4,16,1536]{2,1,0:T(8,128)}, u32[]{:S(2)}) copy-start(f32[4,16,1536]{2,1,0:T(8,128)} %reshape.285) | copy-start | bytes 1179652
  188.8 9.1 %copy-start.13 = (f32[4,16,1536]{2,1,0:T(8,128)S(1)}, f32[4,16,1536]{2,1,0:T(8,128)}, u32[]{:S(2)}) copy-start(f32[4,16,1536]{2,1,0:T(8,128)} %reshape.286) | copy-start | bytes 1179652
  188.8 9.0 %collective-permute-start.19 = (f32[4,16,1536]{2,1,0:T(8,128)S(1)}, f32[4,16,1536]{2,1,0:T(8,128)S(1)}, u32[]{:S(2)}, u32[]{:S(2)}) collective-permute-start(f32[4,16,1536]{2,1,0:T(8,128)S(1)} %select_bitcast_fusion.1), channel_id=1, source_target_pairs={{0,2},{1,3},{2,0},{3,1},{4,6},{5,7},{6,4},{7,5},{8,10},{9,11},{10,... | collective-permute-start | bytes 1179656 | tf_op jit(solution)/shard_map/ppermute | solution.py:182
  198.0 8.9 %copy-start.18 = (f32[16,128]{1,0:T(8,128)S(1)}, f32[16,128]{1,0:T(8,128)}, u32[]{:S(2)}) copy-start(f32[16,128]{1,0:T(8,128)} %get-tuple-element.43) | copy-start | bytes 24580
  198.0 8.9 %copy-start.19 = (f32[16,128]{1,0:T(8,128)S(1)}, f32[16,128]{1,0:T(8,128)}, u32[]{:S(2)}) copy-start(f32[16,128]{1,0:T(8,128)} %get-tuple-element.44) | copy-start | bytes 24580
  198.0 6.2 %collective-permute-start.21 = (f32[2,16,1536]{2,1,0:T(8,128)S(1)}, f32[2,16,1536]{2,1,0:T(8,128)S(1)}, u32[]{:S(2)}, u32[]{:S(2)}) collective-permute-start(f32[2,16,1536]{2,1,0:T(8,128)S(1)} %select_bitcast_fusion.2), channel_id=1, source_target_pairs={{0,4},{1,5},{2,6},{3,7},{4,0},{5,1},{6,2},{7,3},{8,12},{9,13},{10,... | collective-permute-start | bytes 589832 | tf_op jit(solution)/shard_map/ppermute | solution.py:182
  204.3 6.6 %collective-permute-start.23 = (f32[1,16,1536]{2,1,0:T(8,128)S(1)}, f32[1,16,1536]{2,1,0:T(8,128)S(1)}, u32[]{:S(2)}, u32[]{:S(2)}) collective-permute-start(f32[1,16,1536]{2,1,0:T(8,128)S(1)} %select_bitcast_fusion.4), channel_id=1, source_target_pairs={{0,8},{1,9},{2,10},{3,11},{4,12},{5,13},{6,14},{7,15},{8,0},{9,1},... | collective-permute-start | bytes 294920 | tf_op jit(solution)/shard_map/ppermute | solution.py:182
Sparse Core Ops, SparseCore 0:
  10.9 90.9 all-gather.1

commit v2 on v1

--- a/solution.py
+++ b/solution.py
@@ -192,10 +192,400 @@
     return (out, text_out)
 
 
+def fused_kernel(
+    n,
+    meta,
+    q_ref,
+    k_ref,
+    v_ref,
+    qt_ref,
+    kt_ref,
+    vt_ref,
+    bias_all,
+    bias_own,
+    out,
+    text_out,
+    tiles,
+    tq,
+    tkv,
+    part,
+    got_sib,
+    got_pair,
+    got_row,
+    a_send,
+    a_recv,
+    b_send,
+    b_recv,
+    s_send,
+    s_recv,
+    f_send,
+    f_recv,
+    tz_send,
+    tz_recv,
+    ty_send,
+    ty_recv,
+    p_send,
+    p_recv,
+    pz_send,
+    pz_recv,
+):
+    rows, width = q_ref.shape
+    heads = width // HD
+    here = qt_ref.shape[0]
+    nz = n // 4
+    me = lax.axis_index("ctx")
+    core = lax.rem(me, 2)
+    side = lax.rem(me // 2, 2)
+    row = me // 4
+    sib = me + 1 - 2 * core
+    pair = me + 2 - 4 * side
+    far_to = me + 4 - 8 * side
+    has_to = jnp.logical_and(far_to >= 0, far_to < n)
+    far_from = me - 4 + 8 * side
+    has_from = jnp.logical_and(far_from >= 0, far_from < n)
+    from_pair = core == side
+    relay = jnp.where(from_pair, 1, 2)
+    relay_ok = jnp.logical_or(from_pair, has_from)
+    relay_in = jnp.logical_or(core != side, has_from)
+    peers = [lax.rem(row + k, nz) * 4 + side * 2 + core for k in range(1, nz)]
+    sources = [lax.rem(row + nz - k, nz) for k in range(1, nz)]
+    ahead = min(3, heads)
+
+    def col(h):
+        return pl.ds(pl.multiple_of(h * HD, HD), HD)
+
+    def remote(src, dst, send, recv, dev):
+        return pltpu.make_async_remote_copy(
+            src_ref=src,
+            dst_ref=dst,
+            send_sem=send,
+            recv_sem=recv,
+            device_id={"ctx": dev},
+            device_id_type=pl.DeviceIdType.MESH,
+        )
+
+    def copy_a(h):
+        return remote(tiles.at[0, h], tiles.at[1, h], a_send.at[h], a_recv.at[h], pair)
+
+    def copy_b(h):
+        return remote(tiles.at[1, h], tiles.at[2, h], b_send.at[h], b_recv.at[h], far_to)
+
+    def copy_s(h):
+        return remote(tiles.at[0, h], tiles.at[3, h], s_send.at[h], s_recv.at[h], sib)
+
+    def copy_f(h):
+        return remote(tiles.at[relay, h], tiles.at[4, h], f_send.at[h], f_recv.at[h], sib)
+
+    def text_z(buf, i, k):
+        spot = buf.at[core, side, row]
+        return remote(spot, spot, tz_send.at[i, k], tz_recv.at[i, k], peers[k])
+
+    def text_z_wait(buf, i, k):
+        spot = buf.at[core, side, sources[k]]
+        remote(spot, spot, tz_send.at[i, k], tz_recv.at[i, k], peers[k]).wait_recv()
+
+    def text_y(buf, i, mine):
+        spot = buf.at[core, side if mine else 1 - side]
+        return remote(spot, spot, ty_send.at[i, 0], ty_recv.at[i, 0], pair)
+
+    def text_s(buf, i, mine):
+        spot = buf.at[core if mine else 1 - core]
+        return remote(spot, spot, ty_send.at[i, 1], ty_recv.at[i, 1], sib)
+
+    barrier = pltpu.get_barrier_semaphore()
+    for peer in [sib, pair] + peers:
+        pl.semaphore_signal(
+            barrier, inc=1, device_id={"ctx": peer}, device_id_type=pl.DeviceIdType.MESH
+        )
+
+    tq[core, side, row] = qt_ref[...]
+    tkv[core, side, row, 0] = kt_ref[...]
+    tkv[core, side, row, 1] = vt_ref[...]
+
+    def stage_own(h, _):
+        tiles[0, h, 0] = k_ref[:, col(h)]
+        tiles[0, h, 1] = v_ref[:, col(h)]
+        return 0
+
+    lax.fori_loop(0, heads, stage_own, 0)
+    part[:, :, :, :, width:] = jnp.zeros((2, 2, nz, here, 256), jnp.float32)
+    pl.semaphore_wait(barrier, nz + 1)
+
+    for k in range(nz - 1):
+        text_z(tq, 0, k).start()
+    for h in range(ahead):
+        copy_a(h).start()
+        copy_s(h).start()
+    for k in range(nz - 1):
+        text_z(tkv, 1, k).start()
+
+    def relay_step(h):
+        @pl.when(has_from)
+        def _():
+            copy_b(h).wait_recv()
+
+        @pl.when(relay_ok)
+        def _():
+            copy_f(h).start()
+
+    def pump(t):
+        copy_a(t).wait_recv()
+
+        @pl.when(has_to)
+        def _():
+            copy_b(t).start()
+
+        def more():
+            copy_a(t + ahead).start()
+            copy_s(t + ahead).start()
+
+        if isinstance(t, int):
+            if t + ahead < heads:
+                more()
+            if t > 0:
+                relay_step(t - 1)
+        else:
+            pl.when(t + ahead < heads)(more)
+            relay_step(t - 1)
+
+    def text_head(h, _):
+        q = tq[:, :, :, :, col(h)].reshape(n * here, HD)
+        scores = [qk(q, tiles[0, h, 0]), qk(q, kt_ref[:, col(h)]) + bias_own[...]]
+        peak, total, acc = softmax_parts(scores, [tiles[0, h, 1], vt_ref[:, col(h)]])
+        part[:, :, :, :, col(h)] = acc.reshape(2, 2, nz, here, HD)
+        lane = lax.broadcasted_iota(jnp.int32, (n * here, 128), 1) == h
+        for base, value in ((width, peak), (width + 128, total)):
+            old = part[:, :, :, :, base : base + 128].reshape(n * here, 128)
+            new = jnp.where(lane, value, old)
+            part[:, :, :, :, base : base + 128] = new.reshape(2, 2, nz, here, 128)
+        return 0
+
+    lo_far = meta[0] == 2
+    hi_sib = meta[1] == 3
+    hi_fwd = meta[1] == 4
+
+    def video_head(h):
+        copy_s(h).wait_recv()
+
+        @pl.when(relay_in)
+        def _():
+            copy_f(h).wait_recv()
+
+        picked = []
+        for j in range(2):
+            near, far = tiles[1, h, j], tiles[2, h, j]
+            lo = jnp.where(lo_far, far, near)
+            hi = jnp.where(hi_fwd, tiles[4, h, j], jnp.where(hi_sib, tiles[3, h, j], far))
+            words = tkv[:, :, :, j, :, col(h)].reshape(n * here, HD)
+            picked.append((tiles[0, h, j], lo, hi, words))
+        block = 128
+        for r in range(rows // block):
+            qr = q_ref[r * block : (r + 1) * block, col(h)]
+            scores = [qk(qr, key) for key in picked[0]]
+            scores[3] = scores[3] + bias_all[...]
+            _, total, acc = softmax_parts(scores, picked[1])
+            out[r * block : (r + 1) * block, col(h)] = (acc / total).astype(jnp.bfloat16)
+
+    def joined(first, second):
+        peak1, peak2 = first[:, width : width + 128], second[:, width : width + 128]
+        joint = jnp.maximum(peak1, peak2)
+        f1, f2 = jnp.exp2((peak1 - joint) * C2), jnp.exp2((peak2 - joint) * C2)
+        total = first[:, width + 128 :] * f1 + second[:, width + 128 :] * f2
+        pieces = [
+            first[:, h * HD : (h + 1) * HD] * f1[:, h : h + 1]
+            + second[:, h * HD : (h + 1) * HD] * f2[:, h : h + 1]
+            for h in range(heads)
+        ]
+        return pieces + [joint, total]
+
+    def store_joined(view, pieces):
+        for i, piece in enumerate(pieces):
+            view[:, i * 128 : (i + 1) * 128] = piece
+
+    def part_s():
+        return remote(part.at[1 - core], got_sib, p_send.at[0], p_recv.at[0], sib)
+
+    def part_y():
+        return remote(part.at[core, 1 - side], got_pair, p_send.at[1], p_recv.at[1], pair)
+
+    def part_z(k):
+        there = lax.rem(row + k + 1, nz)
+        return remote(
+            part.at[core, side, there], got_row.at[k], pz_send.at[k], pz_recv.at[k], peers[k]
+        )
+
+    pump(0)
+    for k in range(nz - 1):
+        text_z_wait(tq, 0, k)
+    text_y(tq, 0, True).start()
+    pump(1)
+    text_y(tq, 0, False).wait_recv()
+    text_s(tq, 0, True).start()
+    for k in range(nz - 1):
+        text_z_wait(tkv, 1, k)
+    text_y(tkv, 1, True).start()
+    pump(2)
+    text_s(tq, 0, False).wait_recv()
+
+    batch = heads // 4
+
+    def text_batch(i, _):
+        lax.fori_loop(i * batch, (i + 1) * batch, text_head, 0)
+        pump(3 + i)
+        return 0
+
+    lax.fori_loop(0, 4, text_batch, 0)
+    part_s().start()
+    text_y(tkv, 1, False).wait_recv()
+    text_s(tkv, 1, True).start()
+    pump(7)
+    text_s(tkv, 1, False).wait_recv()
+
+    def with_pump(h, _):
+        pump(8 + h)
+        video_head(h)
+        return 0
+
+    def only_video(h, _):
+        video_head(h)
+        return 0
+
+    first = heads - 8
+    lax.fori_loop(0, first, with_pump, 0)
+    relay_step(heads - 1)
+
+    part_s().wait_recv()
+
+    def join_sib(i, _):
+        y, z = i // nz, lax.rem(i, nz)
+        store_joined(part.at[core, y, z], joined(part[core, y, z], got_sib[y, z]))
+        return 0
+
+    lax.fori_loop(0, 2 * nz, join_sib, 0)
+    part_y().start()
+    lax.fori_loop(first, first + 3, only_video, 0)
+    part_y().wait_recv()
+
+    def join_pair(z, _):
+        store_joined(part.at[core, side, z], joined(part[core, side, z], got_pair[z]))
+        return 0
+
+    lax.fori_loop(0, nz, join_pair, 0)
+    for k in range(nz - 1):
+        part_z(k).start()
+    lax.fori_loop(first + 3, heads, only_video, 0)
+    whole = part[core, side, row]
+    for k in range(nz - 1):
+        part_z(k).wait_recv()
+        whole = jnp.concatenate(joined(whole, got_row[k]), axis=1)
+    for h in range(heads):
+        total = whole[:, width + 128 + h : width + 129 + h]
+        text_out[:, h * HD : (h + 1) * HD] = (whole[:, h * HD : (h + 1) * HD] / total).astype(
+            jnp.bfloat16
+        )
+
+    for i, buf in enumerate((tq, tkv)):
+        for k in range(nz - 1):
+            text_z(buf, i, k).wait_send()
+        text_y(buf, i, True).wait_send()
+        text_s(buf, i, True).wait_send()
+    part_s().wait_send()
+    part_y().wait_send()
+    for k in range(nz - 1):
+        part_z(k).wait_send()
+
+    def drain(h, _):
+        copy_a(h).wait_send()
+        copy_s(h).wait_send()
+
+        @pl.when(has_to)
+        def _():
+            copy_b(h).wait_send()
+
+        @pl.when(relay_ok)
+        def _():
+            copy_f(h).wait_send()
+
+        return 0
+
+    lax.fori_loop(0, heads, drain, 0)
+
+
+def fused(qv, kv, vv, qt, kt, vt, key_tiles, tile_owner, text_count):
+    n = lax.axis_size("ctx")
+    me = lax.axis_index("ctx")
+    rows, width = qv.shape
+    heads = width // HD
+    here = qt.shape[0]
+    nz = n // 4
+    tile_count = tile_owner.shape[0]
+    match = key_tiles[0][:, None] == jnp.arange(tile_count, dtype=jnp.int32)[None, :]
+    off = jnp.sum(jnp.where(match, tile_owner[None, :], 0), axis=-1) - me
+    side_sign = jnp.where((me // 2) % 2 == 0, 2, -2)
+    sib_sign = jnp.where(me % 2 == 0, 1, -1)
+    code = jnp.where(
+        off == 0,
+        0,
+        jnp.where(
+            off == side_sign,
+            1,
+            jnp.where(off == -side_sign, 2, jnp.where(off == sib_sign, 3, 4)),
+        ),
+    )
+    hi = jnp.max(code)
+    meta = jnp.stack([jnp.sum(code) - hi, hi]).astype(jnp.int32)
+    limit = text_count[0]
+    number = jnp.arange(n).reshape(nz, 2, 2).transpose(2, 1, 0).reshape(n, 1)
+    place = (number * here + jnp.arange(here)[None, :]).reshape(1, n * here)
+    bias_all = jnp.where(place < limit, 0.0, -jnp.inf).astype(jnp.float32)
+    own_place = me * here + jnp.arange(here)[None, :]
+    bias_own = jnp.where(own_place < limit, 0.0, -jnp.inf).astype(jnp.float32)
+
+    vmem = pl.BlockSpec(memory_space=pltpu.VMEM)
+    dma = pltpu.SemaphoreType.DMA
+    wide = width + 256
+    return pl.pallas_call(
+        functools.partial(fused_kernel, n),
+        in_specs=[pl.BlockSpec(memory_space=pltpu.SMEM)] + [vmem] * 8,
+        out_specs=[vmem, vmem],
+        out_shape=[
+            jax.ShapeDtypeStruct((rows, width), jnp.bfloat16),
+            jax.ShapeDtypeStruct((here, width), jnp.bfloat16),
+        ],
+        scratch_shapes=[
+            pltpu.VMEM((5, heads, 2, rows, HD), jnp.bfloat16),
+            pltpu.VMEM((2, 2, nz, here, width), jnp.bfloat16),
+            pltpu.VMEM((2, 2, nz, 2, here, width), jnp.bfloat16),
+            pltpu.VMEM((2, 2, nz, here, wide), jnp.float32),
+            pltpu.VMEM((2, nz, here, wide), jnp.float32),
+            pltpu.VMEM((nz, here, wide), jnp.float32),
+            pltpu.VMEM((nz - 1, here, wide), jnp.float32),
+        ]
+        + [dma((heads,))] * 8
+        + [dma((2, nz - 1))] * 2
+        + [dma((2, 2))] * 2
+        + [dma((2,))] * 2
+        + [dma((nz - 1,))] * 2,
+        compiler_params=pltpu.CompilerParams(
+            collective_id=0, has_side_effects=True, vmem_limit_bytes=48 << 20
+        ),
+        name="tile_attention",
+    )(meta, qv, kv, vv, qt, kt, vt, bias_all, bias_own)
+
+
+def whole_device(*args):
+    n = lax.axis_size("ctx")
+    rows, width = args[0].shape
+    here = args[3].shape[0]
+    if rows == TILE and n % 4 == 0 and n >= 8 and here % 16 == 0 and width // HD == 12:
+        return fused(*args)
+    return on_device(*args)
+
+
 def solution(mesh):
     split = P(("groups", "ctx"), None)
     return jax.shard_map(
-        on_device,
+        whole_device,
         mesh=mesh,
         in_specs=(split,) * 7 + (P("groups"), P("groups")),
         out_specs=(split, split),

time: 220 us -> 111 us (0.50)
  the two profiles are of different devices: /device:TPU:0 before, /device:TPU:15 now
where the time goes in v2:
time: 111 us
  Pallas kernels  97.8 us (88%)
  local copies, waits for them, and re-layouts  8.01 us (7%)
  between operations  2.65 us (2%)
  other arithmetic  2.3 us (2%)
    pallas_call x1, Pallas kernels, fused(): pl.pallas_call(functools.partial(fused_kernel, n), in_specs=[pl.BlockSpec...  97.8 us
    unnamed x14, local copies, waits for them, and re-layouts  7.85 us

profile of v2, /device:TPU:15, one launch (start us, length us, event | category | flops | bytes accessed | tf_op | source)
XLA Modules:
  0.0 110.8 jit_solution(14892469906318928140)
XLA Ops:
  1.3 0.9 select_reduce_fusion
  2.2 0.6 fusion.1
  4.1 0.7 pad_add_fusion.meta
  4.9 0.1 mul.15
  4.9 0.1 fusion
  5.0 0.1 select_n.61.bias_all
  5.1 0.0 copy-start
  5.1 1.3 %copy-done = bf16[384,1536]{1,0:T(8,128)(2,1)S(1)} copy-done((bf16[384,1536]{1,0:T(8,128)(2,1)S(1)}, bf16[384,1536]{1,0:T(8,128)(2,1)}, u32[]{:S(2)}) %copy-start) | copy-done | bytes 1179672
  6.4 0.0 copy-start.1
  6.4 1.3 %copy-done.1 = bf16[384,1536]{1,0:T(8,128)(2,1)S(1)} copy-done((bf16[384,1536]{1,0:T(8,128)(2,1)S(1)}, bf16[384,1536]{1,0:T(8,128)(2,1)}, u32[]{:S(2)}) %copy-start.1) | copy-done | bytes 1179672
  7.7 0.0 copy-start.2
  7.7 1.3 %copy-done.2 = bf16[384,1536]{1,0:T(8,128)(2,1)S(1)} copy-done((bf16[384,1536]{1,0:T(8,128)(2,1)S(1)}, bf16[384,1536]{1,0:T(8,128)(2,1)}, u32[]{:S(2)}) %copy-start.2) | copy-done | bytes 1179672
  8.9 0.0 copy-start.3
  8.9 0.8 copy-done.3
  9.7 0.0 copy-start.4
  9.7 0.8 copy-done.4
  10.5 0.0 copy-start.5
  10.5 0.8 copy-done.5
  11.3 97.8 %tile_attention.1 = (bf16[384,1536]{1,0:T(8,128)(2,1)S(1)}, bf16[16,1536]{1,0:T(8,128)(2,1)S(1)}) custom-call(s32[2]{0:T(128)S(1)} %pad_add_fusion.meta, bf16[384,1536]{1,0:T(8,128)(2,1)S(1)} %copy-done, bf16[384,1536]{1,0:T(8,128)(2,1)S(1)} %copy-done.1, bf16[384,1536]{1,0:T(8,128)(2,1)S(1)} %copy-done.2, bf16[16,1536]{1,0:T(8,128)(2,1)S(1)} %copy-done.3, ...), custom_call_target="tpu_custom_call" | custom-call | tf_op jit(solution)/shard_map/tile_attention/pallas_call | solution.py:547
  109.1 1.0 copy.14
  110.2 0.6 copy.15
  (2 shorter events, 0.0 us)
Async XLA Ops:
  5.1 1.3 %copy-start = (bf16[384,1536]{1,0:T(8,128)(2,1)S(1)}, bf16[384,1536]{1,0:T(8,128)(2,1)}, u32[]{:S(2)}) copy-start(bf16[384,1536]{1,0:T(8,128)(2,1)} %q_ref.1) | copy-start | bytes 3538948
  6.4 1.3 %copy-start.1 = (bf16[384,1536]{1,0:T(8,128)(2,1)S(1)}, bf16[384,1536]{1,0:T(8,128)(2,1)}, u32[]{:S(2)}) copy-start(bf16[384,1536]{1,0:T(8,128)(2,1)} %k_ref.1) | copy-start | bytes 3538948
  7.7 1.3 %copy-start.2 = (bf16[384,1536]{1,0:T(8,128)(2,1)S(1)}, bf16[384,1536]{1,0:T(8,128)(2,1)}, u32[]{:S(2)}) copy-start(bf16[384,1536]{1,0:T(8,128)(2,1)} %v_ref.1) | copy-start | bytes 3538948
  8.9 0.8 copy-start.3
  9.7 0.8 copy-start.4
  10.5 0.8 copy-start.5

commit v3 on v2

--- a/solution.py
+++ b/solution.py
@@ -194,17 +194,18 @@
 
 def fused_kernel(
     n,
-    meta,
-    q_ref,
-    k_ref,
-    v_ref,
-    qt_ref,
-    kt_ref,
-    vt_ref,
-    bias_all,
-    bias_own,
+    listed,
+    owner,
+    count,
+    q_hbm,
+    k_hbm,
+    v_hbm,
+    qt_hbm,
+    kt_hbm,
+    vt_hbm,
     out,
     text_out,
+    q_ref,
     tiles,
     tq,
     tkv,
@@ -228,10 +229,12 @@
     p_recv,
     pz_send,
     pz_recv,
+    own_sem,
+    in_sem,
 ):
     rows, width = q_ref.shape
     heads = width // HD
-    here = qt_ref.shape[0]
+    here = qt_hbm.shape[0]
     nz = n // 4
     me = lax.axis_index("ctx")
     core = lax.rem(me, 2)
@@ -298,26 +301,58 @@
             barrier, inc=1, device_id={"ctx": peer}, device_id_type=pl.DeviceIdType.MESH
         )
 
-    tq[core, side, row] = qt_ref[...]
-    tkv[core, side, row, 0] = kt_ref[...]
-    tkv[core, side, row, 1] = vt_ref[...]
-
-    def stage_own(h, _):
-        tiles[0, h, 0] = k_ref[:, col(h)]
-        tiles[0, h, 1] = v_ref[:, col(h)]
-        return 0
-
-    lax.fori_loop(0, heads, stage_own, 0)
+    def own_copy(h, j):
+        return pltpu.make_async_copy(
+            (k_hbm, v_hbm)[j].at[:, col(h)], tiles.at[0, h, j], own_sem.at[j, h]
+        )
+
+    text_in = [
+        pltpu.make_async_copy(qt_hbm, tq.at[core, side, row], in_sem.at[0]),
+        pltpu.make_async_copy(kt_hbm, tkv.at[core, side, row, 0], in_sem.at[1]),
+        pltpu.make_async_copy(vt_hbm, tkv.at[core, side, row, 1], in_sem.at[2]),
+    ]
+    query_in = pltpu.make_async_copy(q_hbm, q_ref, in_sem.at[3])
+    for copy in text_in:
+        copy.start()
+
+    def own_start(h, _):
+        own_copy(h, 0).start()
+        own_copy(h, 1).start()
+        return 0
+
+    def own_wait(h, _):
+        own_copy(h, 0).wait()
+        own_copy(h, 1).wait()
+        return 0
+
+    lax.fori_loop(0, heads, own_start, 0)
+    query_in.start()
     part[:, :, :, :, width:] = jnp.zeros((2, 2, nz, here, 256), jnp.float32)
+
+    limit = count[0]
+    spot = lax.broadcasted_iota(jnp.int32, (1, n * here), 1)
+    lane_r = spot & (here - 1)
+    lane_z = (spot >> (here.bit_length() - 1)) & (nz - 1)
+    lane_y = (spot >> ((here * nz).bit_length() - 1)) & 1
+    lane_c = spot >> ((here * nz * 2).bit_length() - 1)
+    place = (lane_z * 4 + lane_y * 2 + lane_c) * here + lane_r
+    bias_all = jnp.where(place < limit, 0.0, -jnp.inf).astype(jnp.float32)
+    own_place = me * here + lax.broadcasted_iota(jnp.int32, (1, here), 1)
+    bias_own = jnp.where(own_place < limit, 0.0, -jnp.inf).astype(jnp.float32)
+
+    for copy in text_in:
+        copy.wait()
     pl.semaphore_wait(barrier, nz + 1)
 
     for k in range(nz - 1):
         text_z(tq, 0, k).start()
+    lax.fori_loop(0, ahead, own_wait, 0)
     for h in range(ahead):
         copy_a(h).start()
         copy_s(h).start()
     for k in range(nz - 1):
         text_z(tkv, 1, k).start()
+    lax.fori_loop(ahead, heads, own_wait, 0)
 
     def relay_step(h):
         @pl.when(has_from)
@@ -350,8 +385,8 @@
 
     def text_head(h, _):
         q = tq[:, :, :, :, col(h)].reshape(n * here, HD)
-        scores = [qk(q, tiles[0, h, 0]), qk(q, kt_ref[:, col(h)]) + bias_own[...]]
-        peak, total, acc = softmax_parts(scores, [tiles[0, h, 1], vt_ref[:, col(h)]])
+        scores = [qk(q, tiles[0, h, 0]), qk(q, tkv[core, side, row, 0, :, col(h)]) + bias_own]
+        peak, total, acc = softmax_parts(scores, [tiles[0, h, 1], tkv[core, side, row, 1, :, col(h)]])
         part[:, :, :, :, col(h)] = acc.reshape(2, 2, nz, here, HD)
         lane = lax.broadcasted_iota(jnp.int32, (n * here, 128), 1) == h
         for base, value in ((width, peak), (width + 128, total)):
@@ -360,9 +395,18 @@
             part[:, :, :, :, base : base + 128] = new.reshape(2, 2, nz, here, 128)
         return 0
 
-    lo_far = meta[0] == 2
-    hi_sib = meta[1] == 3
-    hi_fwd = meta[1] == 4
+    codes = []
+    for j in range(listed.shape[1]):
+        off = owner[listed[0, j]] - me
+        code = jnp.where(off == sib - me, 3, 4)
+        code = jnp.where(off == me - pair, 2, code)
+        code = jnp.where(off == pair - me, 1, code)
+        codes.append(jnp.where(off == 0, 0, code))
+    hi_code = functools.reduce(jnp.maximum, codes)
+    lo_code = sum(codes) - hi_code
+    lo_far = lo_code == 2
+    hi_sib = hi_code == 3
+    hi_fwd = hi_code == 4
 
     def video_head(h):
         copy_s(h).wait_recv()
@@ -382,7 +426,7 @@
         for r in range(rows // block):
             qr = q_ref[r * block : (r + 1) * block, col(h)]
             scores = [qk(qr, key) for key in picked[0]]
-            scores[3] = scores[3] + bias_all[...]
+            scores[3] = scores[3] + bias_all
             _, total, acc = softmax_parts(scores, picked[1])
             out[r * block : (r + 1) * block, col(h)] = (acc / total).astype(jnp.bfloat16)
 
@@ -414,66 +458,60 @@
             part.at[core, side, there], got_row.at[k], pz_send.at[k], pz_recv.at[k], peers[k]
         )
 
-    pump(0)
+    def join_sib(i, _):
+        y, z = i // nz, lax.rem(i, nz)
+        store_joined(part.at[core, y, z], joined(part[core, y, z], got_sib[y, z]))
+        return 0
+
+    def join_pair(z, _):
+        store_joined(part.at[core, side, z], joined(part[core, side, z], got_pair[z]))
+        return 0
+
     for k in range(nz - 1):
         text_z_wait(tq, 0, k)
     text_y(tq, 0, True).start()
-    pump(1)
+    pump(0)
     text_y(tq, 0, False).wait_recv()
     text_s(tq, 0, True).start()
     for k in range(nz - 1):
         text_z_wait(tkv, 1, k)
     text_y(tkv, 1, True).start()
+    pump(1)
+    text_s(tq, 0, False).wait_recv()
+    half = heads // 2
+    lax.fori_loop(0, half, text_head, 0)
     pump(2)
-    text_s(tq, 0, False).wait_recv()
-
-    batch = heads // 4
-
-    def text_batch(i, _):
-        lax.fori_loop(i * batch, (i + 1) * batch, text_head, 0)
-        pump(3 + i)
-        return 0
-
-    lax.fori_loop(0, 4, text_batch, 0)
+    lax.fori_loop(half, heads, text_head, 0)
     part_s().start()
+    pump(3)
     text_y(tkv, 1, False).wait_recv()
     text_s(tkv, 1, True).start()
-    pump(7)
-    text_s(tkv, 1, False).wait_recv()
-
-    def with_pump(h, _):
-        pump(8 + h)
-        video_head(h)
-        return 0
-
-    def only_video(h, _):
-        video_head(h)
-        return 0
-
-    first = heads - 8
-    lax.fori_loop(0, first, with_pump, 0)
-    relay_step(heads - 1)
-
     part_s().wait_recv()
-
-    def join_sib(i, _):
-        y, z = i // nz, lax.rem(i, nz)
-        store_joined(part.at[core, y, z], joined(part[core, y, z], got_sib[y, z]))
-        return 0
-
     lax.fori_loop(0, 2 * nz, join_sib, 0)
     part_y().start()
-    lax.fori_loop(first, first + 3, only_video, 0)
+    pump(4)
+    text_s(tkv, 1, False).wait_recv()
+    query_in.wait()
+
+    def video_pair(i, _):
+        pump(5 + i)
+        lax.fori_loop(2 * i, 2 * i + 2, lambda h, c: (video_head(h), c)[1], 0)
+        return 0
+
+    lax.fori_loop(0, 3, video_pair, 0)
     part_y().wait_recv()
-
-    def join_pair(z, _):
-        store_joined(part.at[core, side, z], joined(part[core, side, z], got_pair[z]))
-        return 0
-
     lax.fori_loop(0, nz, join_pair, 0)
     for k in range(nz - 1):
         part_z(k).start()
-    lax.fori_loop(first + 3, heads, only_video, 0)
+
+    def video_last(i, _):
+        pump(8 + i)
+        video_head(6 + i)
+        return 0
+
+    lax.fori_loop(0, heads - 8, video_last, 0)
+    video_head(heads - 2)
+    relay_step(heads - 1)
     whole = part[core, side, row]
     for k in range(nz - 1):
         part_z(k).wait_recv()
@@ -483,6 +521,7 @@
         text_out[:, h * HD : (h + 1) * HD] = (whole[:, h * HD : (h + 1) * HD] / total).astype(
             jnp.bfloat16
         )
+    video_head(heads - 1)
 
     for i, buf in enumerate((tq, tkv)):
         for k in range(nz - 1):
@@ -513,46 +552,24 @@
 
 def fused(qv, kv, vv, qt, kt, vt, key_tiles, tile_owner, text_count):
     n = lax.axis_size("ctx")
-    me = lax.axis_index("ctx")
     rows, width = qv.shape
     heads = width // HD
     here = qt.shape[0]
     nz = n // 4
-    tile_count = tile_owner.shape[0]
-    match = key_tiles[0][:, None] == jnp.arange(tile_count, dtype=jnp.int32)[None, :]
-    off = jnp.sum(jnp.where(match, tile_owner[None, :], 0), axis=-1) - me
-    side_sign = jnp.where((me // 2) % 2 == 0, 2, -2)
-    sib_sign = jnp.where(me % 2 == 0, 1, -1)
-    code = jnp.where(
-        off == 0,
-        0,
-        jnp.where(
-            off == side_sign,
-            1,
-            jnp.where(off == -side_sign, 2, jnp.where(off == sib_sign, 3, 4)),
-        ),
-    )
-    hi = jnp.max(code)
-    meta = jnp.stack([jnp.sum(code) - hi, hi]).astype(jnp.int32)
-    limit = text_count[0]
-    number = jnp.arange(n).reshape(nz, 2, 2).transpose(2, 1, 0).reshape(n, 1)
-    place = (number * here + jnp.arange(here)[None, :]).reshape(1, n * here)
-    bias_all = jnp.where(place < limit, 0.0, -jnp.inf).astype(jnp.float32)
-    own_place = me * here + jnp.arange(here)[None, :]
-    bias_own = jnp.where(own_place < limit, 0.0, -jnp.inf).astype(jnp.float32)
-
     vmem = pl.BlockSpec(memory_space=pltpu.VMEM)
     dma = pltpu.SemaphoreType.DMA
     wide = width + 256
     return pl.pallas_call(
         functools.partial(fused_kernel, n),
-        in_specs=[pl.BlockSpec(memory_space=pltpu.SMEM)] + [vmem] * 8,
+        in_specs=[pl.BlockSpec(memory_space=pltpu.SMEM)] * 3
+        + [pl.BlockSpec(memory_space=pl.ANY)] * 6,
         out_specs=[vmem, vmem],
         out_shape=[
             jax.ShapeDtypeStruct((rows, width), jnp.bfloat16),
             jax.ShapeDtypeStruct((here, width), jnp.bfloat16),
         ],
         scratch_shapes=[
+            pltpu.VMEM((rows, width), jnp.bfloat16),
             pltpu.VMEM((5, heads, 2, rows, HD), jnp.bfloat16),
             pltpu.VMEM((2, 2, nz, here, width), jnp.bfloat16),
             pltpu.VMEM((2, 2, nz, 2, here, width), jnp.bfloat16),
@@ -565,19 +582,20 @@
         + [dma((2, nz - 1))] * 2
         + [dma((2, 2))] * 2
         + [dma((2,))] * 2
-        + [dma((nz - 1,))] * 2,
+        + [dma((nz - 1,))] * 2
+        + [dma((2, heads)), dma((4,))],
         compiler_params=pltpu.CompilerParams(
-            collective_id=0, has_side_effects=True, vmem_limit_bytes=48 << 20
+            collective_id=0, has_side_effects=True, vmem_limit_bytes=56 << 20
         ),
         name="tile_attention",
-    )(meta, qv, kv, vv, qt, kt, vt, bias_all, bias_own)
+    )(key_tiles, tile_owner, text_count, qv, kv, vv, qt, kt, vt)
 
 
 def whole_device(*args):
     n = lax.axis_size("ctx")
     rows, width = args[0].shape
     here = args[3].shape[0]
-    if rows == TILE and n % 4 == 0 and n >= 8 and here % 16 == 0 and width // HD == 12:
+    if rows == TILE and n % 4 == 0 and n >= 8 and n & (n - 1) == 0 and here in (16, 32, 64) and width // HD == 12:
         return fused(*args)
     return on_device(*args)
 

time: 111 us -> 104 us (0.937)
  local copies, waits for them, and re-layouts: 8.01 us -> 3 us
  other arithmetic: 2.3 us -> 0 us
  between operations: 2.65 us -> 1.3 us
    unnamed x14 -> x4, local copies, waits for them, and re-layouts: 7.85 us -> 3 us
    reduce_sum x2 -> x0, other arithmetic: 1.5 us -> none  [the longest x1 0.85 us: fused(): off = jnp.sum(jnp.where(match, tile_owner[None, :], 0), axis=-1) - me]
where the time goes in v3:
time: 104 us; the launch traced here: 103 us
  Pallas kernels  98.4 us (95%)
  local copies, waits for them, and re-layouts  3 us (3%)
  between operations  1.3 us (1%)
    pallas_call x1, Pallas kernels, fused(): pl.pallas_call(functools.partial(fused_kernel, n), in_specs=[pl.BlockSpec...  98.4 us
    unnamed x4, local copies, waits for them, and re-layouts  3 us

profile of v3, /device:TPU:15, one launch (start us, length us, event | category | flops | bytes accessed | tf_op | source)
XLA Modules:
  0.0 102.7 jit_solution(859873963369903074)
XLA Ops:
  1.3 98.4 %tile_attention.1 = (bf16[384,1536]{1,0:T(8,128)(2,1)}, bf16[16,1536]{1,0:T(8,128)(2,1)}) custom-call(s32[1,3]{1,0:T(1,128)} %listed.1, s32[16]{0:T(128)} %owner.1, s32[1]{0:T(128)S(6)} %copy.13.count, bf16[384,1536]{1,0:T(8,128)(2,1)} %q_hbm.1, bf16[384,1536]{1,0:T(8,128)(2,1)} %k_hbm.1, bf16[384,1536]{1,0:T(8,128)(2,1)} %v_hbm.1, bf16[16,1536]{1,0:T(8,128)(2,1)} %qt_hbm.1, ...), custom_call_target="tpu_custom_call" | custom-call | tf_op jit(solution)/shard_map/tile_attention/pallas_call | solution.py:562
  99.7 0.0 copy-start
  99.7 2.4 %copy.14 = bf16[384,1536]{1,0:T(8,128)(2,1)} copy(bf16[384,1536]{1,0:T(8,128)(2,1)} %get-tuple-element.4) | data formatting | bytes 2359296
  102.1 0.0 copy-done
  102.1 0.6 copy.15
Async XLA Ops:
  99.7 2.4 %copy-start = (bf16[16,1536]{1,0:T(8,128)(2,1)S(1)}, bf16[16,1536]{1,0:T(8,128)(2,1)}, u32[]{:S(2)}) copy-start(bf16[16,1536]{1,0:T(8,128)(2,1)} %get-tuple-element.5) | copy-start | bytes 147460

commit v4 on v3

--- a/solution.py
+++ b/solution.py
@@ -212,6 +212,8 @@
     part,
     got_sib,
     got_pair,
+    pair_stats,
+    sent_pair,
     got_row,
     a_send,
     a_recv,
@@ -450,7 +452,16 @@
         return remote(part.at[1 - core], got_sib, p_send.at[0], p_recv.at[0], sib)
 
     def part_y():
-        return remote(part.at[core, 1 - side], got_pair, p_send.at[1], p_recv.at[1], pair)
+        return remote(sent_pair, got_pair, p_send.at[1], p_recv.at[1], pair)
+
+    def part_ys():
+        return remote(
+            part.at[core, 1 - side, :, :, pl.ds(width, 256)],
+            pair_stats,
+            p_send.at[2],
+            p_recv.at[2],
+            pair,
+        )
 
     def part_z(k):
         there = lax.rem(row + k + 1, nz)
@@ -463,8 +474,13 @@
         store_joined(part.at[core, y, z], joined(part[core, y, z], got_sib[y, z]))
         return 0
 
+    def round_pair(z, _):
+        sent_pair[z] = part[core, 1 - side, z, :, :width].astype(jnp.bfloat16)
+        return 0
+
     def join_pair(z, _):
-        store_joined(part.at[core, side, z], joined(part[core, side, z], got_pair[z]))
+        theirs = jnp.concatenate([got_pair[z].astype(jnp.float32), pair_stats[z]], axis=1)
+        store_joined(part.at[core, side, z], joined(part[core, side, z], theirs))
         return 0
 
     for k in range(nz - 1):
@@ -488,7 +504,9 @@
     text_s(tkv, 1, True).start()
     part_s().wait_recv()
     lax.fori_loop(0, 2 * nz, join_sib, 0)
+    lax.fori_loop(0, nz, round_pair, 0)
     part_y().start()
+    part_ys().start()
     pump(4)
     text_s(tkv, 1, False).wait_recv()
     query_in.wait()
@@ -500,6 +518,7 @@
 
     lax.fori_loop(0, 3, video_pair, 0)
     part_y().wait_recv()
+    part_ys().wait_recv()
     lax.fori_loop(0, nz, join_pair, 0)
     for k in range(nz - 1):
         part_z(k).start()
@@ -530,6 +549,7 @@
         text_s(buf, i, True).wait_send()
     part_s().wait_send()
     part_y().wait_send()
+    part_ys().wait_send()
     for k in range(nz - 1):
         part_z(k).wait_send()
 
@@ -575,13 +595,15 @@
             pltpu.VMEM((2, 2, nz, 2, here, width), jnp.bfloat16),
             pltpu.VMEM((2, 2, nz, here, wide), jnp.float32),
             pltpu.VMEM((2, nz, here, wide), jnp.float32),
-            pltpu.VMEM((nz, here, wide), jnp.float32),
+            pltpu.VMEM((nz, here, width), jnp.bfloat16),
+            pltpu.VMEM((nz, here, 256), jnp.float32),
+            pltpu.VMEM((nz, here, width), jnp.bfloat16),
             pltpu.VMEM((nz - 1, here, wide), jnp.float32),
         ]
         + [dma((heads,))] * 8
         + [dma((2, nz - 1))] * 2
         + [dma((2, 2))] * 2
-        + [dma((2,))] * 2
+        + [dma((3,))] * 2
         + [dma((nz - 1,))] * 2
         + [dma((2, heads)), dma((4,))],
         compiler_params=pltpu.CompilerParams(

time: 104 us -> 99.8 us (0.960)
  Pallas kernels: 98.4 us -> 94.2 us
    pallas_call x1, Pallas kernels: 98.4 us -> 94.2 us  [fused(): pl.pallas_call(functools.partial(fused_kernel, n), in_specs=[pl.BlockSpec...]
where the time goes in v4:
time: 99.8 us; the launch traced here: 98.5 us
  Pallas kernels  94.2 us (94%)
  local copies, waits for them, and re-layouts  3 us (3%)
  between operations  1.3 us (1%)
    pallas_call x1, Pallas kernels, fused(): pl.pallas_call(functools.partial(fused_kernel, n), in_specs=[pl.BlockSpec...  94.2 us
    unnamed x4, local copies, waits for them, and re-layouts  3 us

profile of v4, /device:TPU:15, one launch (start us, length us, event | category | flops | bytes accessed | tf_op | source)
XLA Modules:
  0.0 98.5 jit_solution(5265508647886255353)
XLA Ops:
  1.3 94.2 %tile_attention.1 = (bf16[384,1536]{1,0:T(8,128)(2,1)}, bf16[16,1536]{1,0:T(8,128)(2,1)}) custom-call(s32[1,3]{1,0:T(1,128)} %listed.1, s32[16]{0:T(128)} %owner.1, s32[1]{0:T(128)S(6)} %copy.13.count, bf16[384,1536]{1,0:T(8,128)(2,1)} %q_hbm.1, bf16[384,1536]{1,0:T(8,128)(2,1)} %k_hbm.1, bf16[384,1536]{1,0:T(8,128)(2,1)} %v_hbm.1, bf16[16,1536]{1,0:T(8,128)(2,1)} %qt_hbm.1, ...), custom_call_target="tpu_custom_call" | custom-call | tf_op jit(solution)/shard_map/tile_attention/pallas_call | solution.py:582
  95.5 0.0 copy-start
  95.5 2.4 %copy.14 = bf16[384,1536]{1,0:T(8,128)(2,1)} copy(bf16[384,1536]{1,0:T(8,128)(2,1)} %get-tuple-element.4) | data formatting | bytes 2359296
  97.9 0.0 copy-done
  97.9 0.6 copy.15
Async XLA Ops:
  95.5 2.4 %copy-start = (bf16[16,1536]{1,0:T(8,128)(2,1)S(1)}, bf16[16,1536]{1,0:T(8,128)(2,1)}, u32[]{:S(2)}) copy-start(bf16[16,1536]{1,0:T(8,128)(2,1)} %get-tuple-element.5) | copy-start | bytes 147460
